TPU v7x, 256 devices: a whole 4x4x8 slice. The times are simulated.
256 devices in a mesh: dp: 2 (over core), tm: 32 (over z, y), space: 4 (over x).
Axes of the slice: x: 4, y: 4, z: 8, core: 2. Of those that a mesh axis runs over, the one named last changes fastest.
Arguments:
- latents: bfloat16 [2, 64, 8, 80, 512], P('dp', 'tm', 'space'), may hold values from -6 to 6
- norm_gain: float32 [512], replicated, may hold values from 0.25 to 1.75
- kernel: bfloat16 [13824, 512], P(None, 'dp'), may hold values from -0.0546875 to 0.0546875
- conv_bias: float32 [512], replicated, may hold values from -3 to 3
- out_grad: bfloat16 [2, 64, 8, 80, 512], P('dp', 'tm', 'space'), may hold values from -6 to 6
Outputs:
- block_out: bfloat16 [2, 64, 8, 80, 512], P('dp', 'tm', 'space')
- latent_grad: bfloat16 [2, 64, 8, 80, 512], P('dp', 'tm', 'space')
- kernel_grad: float32 [13824, 512], P('tm', 'dp')
- gain_grad: float32 [512], replicated
- bias_grad: float32 [512], replicated
All inputs are finite; a program needn't handle non-finite values.
Results may differ from a plain program's by a relative error of at most 0.0029.
Values may be sent and summed in bfloat16 or wider, within the bound.
No kernel may reach another device: no remote copies, remote signals or barrier semaphores. Data moves between devices by JAX's collectives and lax.ppermute only.
A program may use at most 128 MiB of HBM per device.

v0:
```python
import jax
import jax.numpy as jnp
from jax import lax
from jax.sharding import PartitionSpec as P


def shifted(block, axis, distance):
    devices = range(lax.axis_size(axis))
    route = [(i - distance, i) for i in devices if i - distance in devices]
    return lax.ppermute(block, axis, route)


def padded(block, sides, width):
    for axis, dim in sides:
        count = lax.axis_size(axis)
        forward = [(i, i + 1) for i in range(count - 1)]
        backward = [(target, source) for source, target in forward]
        low = lax.ppermute(
            lax.slice_in_dim(block, block.shape[dim] - width, None, axis=dim), axis, forward
        )
        high = lax.ppermute(lax.slice_in_dim(block, 0, width, axis=dim), axis, backward)
        block = jnp.concatenate([low, block, high], axis=dim)
    return block


def tap_columns(extended, frame_count, row_count, col_count, flipped):
    pieces = []
    for tap_t in range(3):
        for tap_h in range(3):
            for tap_w in range(3):
                if flipped:
                    start_t, start_h, start_w = (2 - tap_t, 2 - tap_h, 2 - tap_w)
                else:
                    start_t, start_h, start_w = (tap_t, tap_h, tap_w)
                pieces.append(
                    extended[
                        :,
                        start_t : start_t + frame_count,
                        start_h : start_h + row_count,
                        start_w : start_w + col_count,
                        :,
                    ]
                )
    stacked = jnp.concatenate(pieces, axis=-1)
    return stacked.reshape(-1, stacked.shape[-1])


def pad_columns(extended):
    return jnp.pad(extended, ((0, 0), (0, 0), (0, 0), (1, 1), (0, 0)))


def on_device(latents, norm_gain, kernel, conv_bias, out_grad):
    chans = latents.shape[-1]
    half_cols = kernel.shape[1]
    clip_local, frame_count, row_count, col_count = (
        latents.shape[0],
        latents.shape[1],
        latents.shape[2],
        latents.shape[3],
    )
    cell_total = (
        clip_local
        * frame_count
        * row_count
        * col_count
        * lax.axis_size("dp")
        * lax.axis_size("tm")
        * lax.axis_size("space")
    )
    grad_scale = 1.0 / jnp.sqrt(jnp.float32(cell_total))
    floats = latents.astype(jnp.float32)
    scale = lax.rsqrt(jnp.mean(floats * floats, axis=-1, keepdims=True) + 1e-06)
    normed = floats * scale
    pre_act = normed * norm_gain
    act = jax.nn.silu(pre_act).astype(jnp.bfloat16)
    grad_pair = lax.all_to_all(out_grad, "dp", split_axis=4, concat_axis=0, tiled=True)
    earlier = shifted(act, "tm", 1)
    joined = jnp.concatenate([earlier, act], axis=1)
    act_ext = padded(joined, (("space", 2),), 1)
    later = shifted(grad_pair, "tm", -1)
    joined_grad = jnp.concatenate([grad_pair, later], axis=1)
    grad_ext = padded(joined_grad, (("space", 2),), 1)
    act_pair = lax.all_gather(act_ext, "dp", axis=0, tiled=True)
    pair_clips = act_pair.shape[0]
    act_taps = tap_columns(pad_columns(act_pair), frame_count, row_count, col_count, False)
    conv_part = jnp.dot(act_taps, kernel, preferred_element_type=jnp.float32)
    conv_part = conv_part.reshape(pair_clips, frame_count, row_count, col_count, half_cols)
    conv = lax.all_to_all(conv_part, "dp", split_axis=0, concat_axis=4, tiled=True)
    block_out = (floats + conv + conv_bias).astype(jnp.bfloat16)
    kernel_local = (
        lax.dot_general(
            act_taps,
            grad_pair.reshape(-1, half_cols),
            (((0,), (0,)), ((), ())),
            preferred_element_type=jnp.float32,
        )
        * grad_scale
    )
    flipped_kernel = jnp.transpose(kernel.reshape(-1, chans, half_cols), (0, 2, 1)).reshape(
        -1, chans
    )
    grad_taps = tap_columns(pad_columns(grad_ext), frame_count, row_count, col_count, True)
    partial_grad = jnp.dot(grad_taps, flipped_kernel, preferred_element_type=jnp.float32)
    partial_grad = partial_grad.reshape(pair_clips, frame_count, row_count, col_count, chans)
    act_grad = lax.psum_scatter(partial_grad, "dp", scatter_dimension=0, tiled=True)
    grads = out_grad.astype(jnp.float32)
    bias_local = jnp.sum(grads.reshape(-1, chans), axis=0) * grad_scale
    sig = jax.nn.sigmoid(pre_act)
    pre_grad = act_grad * sig * (1.0 + pre_act * (1.0 - sig))
    gain_local = jnp.sum((pre_grad * normed).reshape(-1, chans), axis=0) * grad_scale
    normed_grad = pre_grad * norm_gain
    latent_grad = grads + scale * (
        normed_grad - normed * jnp.mean(normed_grad * normed, axis=-1, keepdims=True)
    )
    gain_grad, bias_grad = lax.psum((gain_local, bias_local), ("dp", "tm", "space"))
    row_part = lax.psum_scatter(kernel_local, "tm", scatter_dimension=0, tiled=True)
    kernel_grad = lax.psum(row_part, "space")
    return (block_out, latent_grad.astype(jnp.bfloat16), kernel_grad, gain_grad, bias_grad)


def solution(mesh):
    in_specs = (
        P("dp", "tm", "space", None, None),
        P(),
        P(None, "dp"),
        P(),
        P("dp", "tm", "space", None, None),
    )
    out_specs = (
        P("dp", "tm", "space", None, None),
        P("dp", "tm", "space", None, None),
        P("tm", "dp"),
        P(),
        P(),
    )
    return jax.shard_map(
        on_device, mesh=mesh, in_specs=in_specs, out_specs=out_specs, check_vma=False
    )
```

profile of v0, /device:TPU:34, one launch (start us, length us, event | category | flops | bytes accessed | tf_op | source)
XLA Modules:
  0.0 440.5 jit_solution(11372110334327910266)
XLA Ops:
  7.2 1.3 copy.20
  8.5 4.2 all_to_all.36
  12.6 0.4 copy.22
  13.0 4.5 %collective-permute-start.3 = (bf16[2,2,2,80,256]{4,3,2,1,0:T(8,128)(2,1)S(1)}, bf16[2,2,2,80,256]{4,3,2,1,0:T(8,128)(2,1)S(1)}, u32[]{:S(2)}, u32[]{:S(2)}) collective-permute-start(bf16[2,2,2,80,256]{4,3,2,1,0:T(8,128)(2,1)S(1)} %bitcast.31), channel_id=1, source_target_pairs={{4,0},{8,4},{12,8},{16,12},{20,16},{24,20},{28,24},{32,28},{36,32}... | collective-permute-start | bytes 983048 | tf_op jit(solution)/shard_map/ppermute | solution.py:10
  17.5 7.2 %collective-permute-done.3 = bf16[2,2,2,80,256]{4,3,2,1,0:T(8,128)(2,1)S(1)} collective-permute-done((bf16[2,2,2,80,256]{4,3,2,1,0:T(8,128)(2,1)S(1)}, bf16[2,2,2,80,256]{4,3,2,1,0:T(8,128)(2,1)S(1)}, u32[]{:S(2)}, u32[]{:S(2)}) %collective-permute-start.3) | collective-permute-done | bytes 327712 | tf_op jit(solution)/shard_map/ppermute | solution.py:10
  24.8 3.4 collective-permute-start.4
  28.2 2.5 collective-permute-start.5
  30.7 10.3 %copy.23 = bf16[27,256,512]{2,1,0:T(8,128)(2,1)} copy(bf16[27,256,512]{1,2,0:T(8,128)(2,1)} %bitcast.37) | data formatting | bytes 14155776 | tf_op jit(solution)/shard_map/transpose | solution.py:99
  41.0 0.7 select_maximum_fusion
  41.7 0.1 slice_dynamic-update-slice_fusion.50
  41.8 0.1 maximum_maximum_fusion
  42.0 0.1 slice_dynamic-update-slice_fusion.47
  42.2 0.1 slice_dynamic-update-slice_fusion.45
  42.4 0.1 slice_dynamic-update-slice_fusion.42
  42.5 0.1 slice_dynamic-update-slice_fusion.39
  42.7 0.1 slice_dynamic-update-slice_fusion.37
  42.8 0.1 slice_dynamic-update-slice_fusion.34
  43.0 0.1 slice_dynamic-update-slice_fusion.31
  43.1 0.1 slice_dynamic-update-slice_fusion.29
  43.3 0.9 slice-done
  44.2 1.1 slice-done.1
  45.2 5.8 %fusion.31 = f32[2,2,2,80,512]{4,3,2,1,0:T(8,128)} fusion(bf16[2,2,2,80,6912]{4,3,2,1,0:T(8,128)(2,1)S(1)} %slice_dynamic-update-slice_fusion.27, bf16[6912,512,1,1,1]{1,0,4,3,2:T(8,128)(2,1)S(1)} %bitcast.40), kind=kOutput, calls=%fused_computation.109 | convolution fusion | flops 4529848320 | bytes 17235968 | tf_op jit(solution)/shard_map/dot_general | solution.py:103
  51.1 0.2 fusion.24
  51.3 18.5 %reduce-scatter.3.cloned.1.call-done = f32[1,2,2,80,512]{4,3,2,1,0:T(8,128)} async-done(((f32[2,2,2,80,512]{4,3,2,1,0:T(8,128)}), f32[1,2,2,80,512]{4,3,2,1,0:T(8,128)}) %reduce-scatter.3.cloned.1.call-update) | async-done | bytes 655376 | tf_op jit(solution)/shard_map/reduce_scatter | solution.py:105
  69.8 1.6 fusion.23
  71.4 2.4 fusion.13
  73.8 3.4 collective-permute-start
  77.2 10.4 %collective-permute-done = bf16[1,2,2,80,512]{4,3,2,1,0:T(8,128)(2,1)S(1)} collective-permute-done((bf16[1,2,2,80,512]{4,3,2,1,0:T(8,128)(2,1)S(1)}, bf16[1,2,2,80,512]{4,3,2,1,0:T(8,128)(2,1)S(1)}, u32[]{:S(2)}, u32[]{:S(2)}) %collective-permute-start) | collective-permute-done | bytes 327712 | tf_op jit(solution)/shard_map/ppermute | solution.py:10
  87.6 3.4 collective-permute-start.1
  91.0 2.5 collective-permute-start.2
  93.5 5.0 %collective-permute-done.1 = bf16[1,4,1,80,512]{4,3,2,1,0:T(8,128)(2,1)S(1)} collective-permute-done((bf16[1,4,1,80,512]{4,3,2,1,0:T(8,128)(2,1)S(1)}, bf16[1,4,1,80,512]{4,3,2,1,0:T(8,128)(2,1)S(1)}, u32[]{:S(2)}, u32[]{:S(2)}) %collective-permute-start.1) | collective-permute-done | bytes 327712 | tf_op jit(solution)/shard_map/ppermute | solution.py:18
  98.4 3.1 collective-permute-done.2
  101.6 1.2 pad_maximum_fusion
  102.8 0.2 reduce-scatter.5.cloned.1.call-start
  103.0 16.3 %all-gather.2.cloned.1.call-done = bf16[2,4,4,80,512]{4,3,2,1,0:T(8,128)(2,1)} async-done(((bf16[1,4,4,80,512]{4,3,2,1,0:T(8,128)(2,1)}), bf16[2,4,4,80,512]{4,3,2,1,0:T(8,128)(2,1)}) %all-gather.2.cloned.1.call-update) | async-done | bytes 2621456 | tf_op jit(solution)/shard_map/all_gather | solution.py:83
  119.4 1.4 slice_dynamic-update-slice_fusion.26
  120.7 1.1 slice_dynamic-update-slice_fusion.8
  121.9 1.2 slice_dynamic-update-slice_fusion.25
  123.1 0.2 slice_dynamic-update-slice_fusion.24
  123.3 0.2 slice_dynamic-update-slice_fusion.23
  123.5 0.2 slice_dynamic-update-slice_fusion.22
  123.7 0.2 slice_dynamic-update-slice_fusion.21
  123.9 0.2 slice_dynamic-update-slice_fusion.20
  124.1 0.2 slice_dynamic-update-slice_fusion.19
  124.3 0.2 slice_dynamic-update-slice_fusion.18
  124.5 0.2 slice_dynamic-update-slice_fusion.17
  124.6 0.2 slice_dynamic-update-slice_fusion.16
  124.8 0.2 slice_dynamic-update-slice_fusion.15
  125.0 0.2 slice_dynamic-update-slice_fusion.14
  125.2 0.2 slice_dynamic-update-slice_fusion.13
  125.4 0.2 slice_dynamic-update-slice_fusion.12
  125.6 0.2 slice_dynamic-update-slice_fusion.11
  125.8 0.2 slice_dynamic-update-slice_fusion.10
  126.0 0.2 slice_dynamic-update-slice_fusion.9
  126.1 6.1 %copy-done.3 = bf16[2,2,2,80,13824]{4,3,2,1,0:T(8,128)(2,1)} copy-done((bf16[2,2,2,80,13824]{4,3,2,1,0:T(8,128)(2,1)}, bf16[2,2,2,80,13824]{4,3,2,1,0:T(8,128)(2,1)S(1)}, u32[]{:S(2)}) %copy-start.3) | copy-done | bytes 17694744
  132.2 9.0 %convolution_multiply_fusion = f32[13824,256]{1,0:T(8,128)} fusion(bf16[640,13824]{1,0:T(8,128)(2,1)S(1)} %bitcast.44, bf16[640,256]{1,0:T(8,128)(2,1)S(1)} %bitcast.36), kind=kOutput, calls=%fused_computation | convolution fusion | flops 4533387264 | bytes 32178176 | tf_op jit(solution)/shard_map/dot_general | solution.py:91
  141.3 76.5 %all-reduce.2 = (f32[512]{0:T(512)}, f32[512]{0:T(512)}) all-reduce(f32[512]{0:T(512)S(1)} %broadcast_multiply_fusion.1, f32[512]{0:T(512)S(1)} %broadcast_multiply_fusion), channel_id=1, replica_groups=mesh['dp'=2,'tm'=32,'space'=4] {'dp','tm','space'}, use_global_device_ids=true, to_apply=%region_6.7 | all-reduce | flops 1024 | bytes 8192 | tf_op jit(solution)/shard_map/psum | solution.py:115
  217.7 166.5 %reduce-scatter.5.cloned.1.call-done = f32[432,256]{1,0:T(8,128)} async-done(((f32[13824,256]{1,0:T(8,128)}), f32[432,256]{1,0:T(8,128)}) %reduce-scatter.5.cloned.1.call-update) | async-done | bytes 442384 | tf_op jit(solution)/shard_map/reduce_scatter | solution.py:116
  384.2 10.5 %fusion = f32[2,2,2,80,256]{4,3,2,1,0:T(8,128)S(1)} fusion(bf16[2,2,2,80,13824]{4,3,2,1,0:T(8,128)(2,1)} %copy-done.3, bf16[13824,256]{1,0:T(8,128)(2,1)} %param.7), kind=kOutput, calls=%fused_computation.1 | convolution fusion | flops 4529848320 | bytes 25427968 | tf_op jit(solution)/shard_map/dot_general | solution.py:86
  394.8 4.3 all_to_all.37
  399.0 0.1 copy.28
  399.1 0.8 fusion.26
  399.9 32.3 %all-reduce.5.cloned.1.call-done = f32[432,256]{1,0:T(8,128)} async-done(((f32[432,256]{1,0:T(8,128)}), f32[432,256]{1,0:T(8,128)}) %all-reduce.5.cloned.1.call-update) | async-done | bytes 442384 | tf_op jit(solution)/shard_map/psum | solution.py:117
  432.2 1.8 copy.82
  (55 shorter events, 1.1 us)
Async XLA Ops:
  7.2 62.6 %reduce-scatter.3.cloned.1.call-start = ((), (), s32[]{:S(2)}) async-start(), calls=%async_computation.5 | async-start | bytes 1966080 | tf_op jit(solution)/shard_map/reduce_scatter | solution.py:105
  13.0 11.7 %collective-permute-start.3 = (bf16[2,2,2,80,256]{4,3,2,1,0:T(8,128)(2,1)S(1)}, bf16[2,2,2,80,256]{4,3,2,1,0:T(8,128)(2,1)S(1)}, u32[]{:S(2)}, u32[]{:S(2)}) collective-permute-start(bf16[2,2,2,80,256]{4,3,2,1,0:T(8,128)(2,1)S(1)} %bitcast.31), channel_id=1, source_target_pairs={{4,0},{8,4},{12,8},{16,12},{20,16},{24,20},{28,24},{32,28},{36,32}... | collective-permute-start | bytes 983048 | tf_op jit(solution)/shard_map/ppermute | solution.py:10
  24.8 16.2 %collective-permute-start.4 = (bf16[2,4,1,80,256]{4,3,2,1,0:T(8,128)(2,1)S(1)}, bf16[2,4,1,80,256]{4,3,2,1,0:T(8,128)(2,1)S(1)}, u32[]{:S(2)}, u32[]{:S(2)}) collective-permute-start(bf16[2,4,1,80,256]{4,3,2,1,0:T(8,128)(2,1)S(1)} %get-tuple-element.11), channel_id=1, source_target_pairs={{0,1},{1,2},{2,3},{4,5},{5,6},{6,7},{8,9},{9,10},{10,11},{12,13},{... | collective-permute-start | bytes 983048 | tf_op jit(solution)/shard_map/ppermute | solution.py:18
  28.2 12.8 %collective-permute-start.5 = (bf16[2,4,1,80,256]{4,3,2,1,0:T(8,128)(2,1)S(1)}, bf16[2,4,1,80,256]{4,3,2,1,0:T(8,128)(2,1)S(1)}, u32[]{:S(2)}, u32[]{:S(2)}) collective-permute-start(bf16[2,4,1,80,256]{4,3,2,1,0:T(8,128)(2,1)S(1)} %get-tuple-element.12), channel_id=1, source_target_pairs={{1,0},{2,1},{3,2},{5,4},{6,5},{7,6},{9,8},{10,9},{11,10},{13,12},{... | collective-permute-start | bytes 983048 | tf_op jit(solution)/shard_map/ppermute | solution.py:21
  42.0 2.2 slice-start
  42.6 2.6 slice-start.1
  45.2 5.9 %copy-start.1 = (bf16[1,2,2,80,512]{4,3,2,1,0:T(8,128)(2,1)S(1)}, bf16[1,2,2,80,512]{4,3,2,1,0:T(8,128)(2,1)}, u32[]{:S(2)}) copy-start(bf16[1,2,2,80,512]{4,3,2,1,0:T(8,128)(2,1)} %param.5) | copy-start | bytes 983044
  45.2 24.5 %copy-start.4 = (f32[512]{0:T(512)S(1)}, f32[512]{0:T(512)}, u32[]{:S(2)}) copy-start(f32[512]{0:T(512)} %param.6) | copy-start | bytes 6148
  45.2 26.2 %copy-start.2 = (bf16[1,2,2,80,512]{4,3,2,1,0:T(8,128)(2,1)S(1)}, bf16[1,2,2,80,512]{4,3,2,1,0:T(8,128)(2,1)}, u32[]{:S(2)}) copy-start(bf16[1,2,2,80,512]{4,3,2,1,0:T(8,128)(2,1)} %param.9) | copy-start | bytes 983044
  51.1 68.3 %all-gather.2.cloned.1.call-start = ((), (), s32[]{:S(2)}) async-start(), calls=%async_computation.4 | async-start | bytes 3932160 | tf_op jit(solution)/shard_map/all_gather | solution.py:83
  73.8 13.8 %collective-permute-start = (bf16[1,2,2,80,512]{4,3,2,1,0:T(8,128)(2,1)S(1)}, bf16[1,2,2,80,512]{4,3,2,1,0:T(8,128)(2,1)S(1)}, u32[]{:S(2)}, u32[]{:S(2)}) collective-permute-start(bf16[1,2,2,80,512]{4,3,2,1,0:T(8,128)(2,1)S(1)} %get-tuple-element.16), channel_id=1, source_target_pairs={{0,4},{4,8},{8,12},{12,16},{16,20},{20,24},{24,28},{28,32},{32,36}... | collective-permute-start | bytes 983048 | tf_op jit(solution)/shard_map/ppermute | solution.py:10
  87.6 10.8 %collective-permute-start.1 = (bf16[1,4,1,80,512]{4,3,2,1,0:T(8,128)(2,1)S(1)}, bf16[1,4,1,80,512]{4,3,2,1,0:T(8,128)(2,1)S(1)}, u32[]{:S(2)}, u32[]{:S(2)}) collective-permute-start(bf16[1,4,1,80,512]{4,3,2,1,0:T(8,128)(2,1)S(1)} %get-tuple-element.13), channel_id=1, source_target_pairs={{0,1},{1,2},{2,3},{4,5},{5,6},{6,7},{8,9},{9,10},{10,11},{12,13},{... | collective-permute-start | bytes 983048 | tf_op jit(solution)/shard_map/ppermute | solution.py:18
  91.0 10.5 %collective-permute-start.2 = (bf16[1,4,1,80,512]{4,3,2,1,0:T(8,128)(2,1)S(1)}, bf16[1,4,1,80,512]{4,3,2,1,0:T(8,128)(2,1)S(1)}, u32[]{:S(2)}, u32[]{:S(2)}) collective-permute-start(bf16[1,4,1,80,512]{4,3,2,1,0:T(8,128)(2,1)S(1)} %get-tuple-element.14), channel_id=1, source_target_pairs={{1,0},{2,1},{3,2},{5,4},{6,5},{7,6},{9,8},{10,9},{11,10},{13,12},{... | collective-permute-start | bytes 983048 | tf_op jit(solution)/shard_map/ppermute | solution.py:21
  102.8 281.4 %reduce-scatter.5.cloned.1.call-start = ((), (), s32[]{:S(2)}) async-start(), calls=%async_computation.6 | async-start | bytes 14598144 | tf_op jit(solution)/shard_map/reduce_scatter | solution.py:116
  119.4 3.8 copy-start
  126.1 6.1 %copy-start.3 = (bf16[2,2,2,80,13824]{4,3,2,1,0:T(8,128)(2,1)}, bf16[2,2,2,80,13824]{4,3,2,1,0:T(8,128)(2,1)S(1)}, u32[]{:S(2)}) copy-start(bf16[2,2,2,80,13824]{4,3,2,1,0:T(8,128)(2,1)S(1)} %slice_dynamic-update-slice_fusion.9) | copy-start | bytes 53084164
  141.2 291.0 %all-reduce.5.cloned.1.call-start = ((), (), s32[]{:S(2)}) async-start(), calls=%async_computation.7 | async-start | bytes 884736 | tf_op jit(solution)/shard_map/psum | solution.py:117
  384.2 14.9 %copy-start.5 = (f32[512]{0:T(512)S(1)}, f32[512]{0:T(512)}, u32[]{:S(2)}) copy-start(f32[512]{0:T(512)} %param.8) | copy-start | bytes 6148
Sparse Core Ops, SparseCore 0:
  51.2 18.5 reduce-scatter.2
  102.9 16.3 all-gather.1
  141.3 242.8 reduce-scatter.4
  386.4 45.7 all-reduce.4
where the time goes:
time: 443 us; the launch traced here: 441 us
  waiting for transfers between devices  259 us (58%)
  blocking collectives  84.9 us (19%)
  local copies, waits for them, and re-layouts  29.6 us (7%)
  matrix products  25.3 us (6%)
  starting transfers between devices  19.9 us (4%)
  between operations  14.4 us (3%)
  other arithmetic  7.21 us (2%)
    reduce_scatter x1, waiting for transfers between devices, on_device(): lax.psum_scatter(kernel_local, 'tm', scatter_dimension=0, tiled=True)  166 us
    psum x1, blocking collectives, on_device(): lax.psum((gain_local, bias_local), ('dp', 'tm', 'space'))  76.5 us
    psum x1, waiting for transfers between devices, on_device(): kernel_grad = lax.psum(row_part, 'space')  32.3 us
    unnamed x69, local copies, waits for them, and re-layouts  18.6 us
    reduce_scatter x1, waiting for transfers between devices, on_device(): lax.psum_scatter(partial_grad, 'dp', scatter_dimension=0, tiled=True)  18.5 us
    ppermute x2, waiting for transfers between devices, shifted(): return lax.ppermute(block, axis, route)  17.6 us
    all_gather x1, waiting for transfers between devices, on_device(): act_pair = lax.all_gather(act_ext, 'dp', axis=0, tiled=True)  16.3 us
    dot_general x1, matrix products, on_device(): conv_part = jnp.dot(act_taps, kernel, preferred_element_type=jnp.float32)  10.5 us
  transfers between devices with their start and end apart: 10, of which 8 were waited for; matrix products, arithmetic and copies ran while one was open for 5% of the time, Pallas kernels for 0%

commit v1 on v0

v1 whole, which is shorter than its diff:
```python
import jax
import jax.numpy as jnp
from jax import lax
from jax.experimental import pallas as pl
from jax.experimental.pallas import tpu as pltpu
from jax.sharding import Mesh, PartitionSpec as P

F32 = jnp.float32
BF16 = jnp.bfloat16
COLS = 80
CH = 512
HALF = 256
CELLS = 320
TOTAL = 81920
EPS = 1e-06
BIG = pltpu.CompilerParams(vmem_limit_bytes=58 * 1024 * 1024)
AXES = {"dp": 2, "z": 8, "y": 4, "x": 4}


def class_of(block, k):
    return jnp.concatenate(
        [block[:, 64 * k : 64 * k + 64], block[:, HALF + 64 * k : HALF + 64 * k + 64]], axis=-1
    )


def normalised(floats):
    scale = 1.0 / jnp.sqrt(jnp.mean(floats * floats, axis=-1, keepdims=True) + EPS)
    return scale, floats * scale


def act_kernel(lat_ref, gain_ref, grad_ref, act_ref, mix_ref):
    for j in range(4):
        rows = pl.ds(COLS * j, COLS)
        floats = lat_ref[rows, :].astype(F32)
        _, normed = normalised(floats)
        pre_act = normed * gain_ref[...]
        act = pre_act / (1.0 + jnp.exp(-pre_act))
        act_ref[rows, :] = act.astype(BF16)
        grad = grad_ref[rows, :].astype(F32)
        for k in range(4):
            act_piece = class_of(act, k).astype(BF16)
            grad_piece = class_of(grad, k).astype(BF16)
            for other in range(4):
                mix_ref[4 * other + k, 0, rows, :] = act_piece
                mix_ref[4 * k + other, 1, rows, :] = grad_piece


def shifted_columns(block):
    wide = block.astype(F32)
    column = lax.broadcasted_iota(jnp.int32, wide.shape, 0)
    before = jnp.where(column == 0, 0.0, pltpu.roll(wide, 1, 0)).astype(BF16)
    after = jnp.where(column == COLS - 1, 0.0, pltpu.roll(wide, COLS - 1, 0)).astype(BF16)
    return before, block, after


def conv_kernel(
    lat_ref, bias_ref, act_ref, prev_ref, low_ref, high_ref, own_ref, oth_ref, out_ref, ext, acc
):
    step = pl.program_id(0)

    @pl.when(step == 0)
    def _():
        for f in range(4):
            for r in range(4):
                if r == 0:
                    block = low_ref[f]
                elif r == 3:
                    block = high_ref[f]
                elif f < 2:
                    block = prev_ref[f, r - 1]
                else:
                    block = act_ref[f - 2, r - 1]
                for s, shifted in enumerate(shifted_columns(block)):
                    ext[s, f, r] = shifted
        acc[...] = jnp.zeros_like(acc)

    tap_t, tap_h = step // 3, step % 3
    window = jnp.concatenate(
        [ext[c, pl.ds(tap_t, 2), pl.ds(tap_h, 2)].reshape(CELLS, CH) for c in range(3)], axis=-1
    )
    acc[0] += jnp.dot(window, own_ref[...], preferred_element_type=F32)
    acc[1] += jnp.dot(window, oth_ref[...], preferred_element_type=F32)

    @pl.when(step == 8)
    def _():
        me = lax.axis_index("dp")
        for half in range(2):
            first = half * HALF
            chans = pl.ds(first, HALF)
            conv = jnp.where(me == half, acc[0], acc[1])
            out_ref[:, chans] = (
                lat_ref[:, chans].astype(F32) + conv + bias_ref[:, chans]
            ).astype(BF16)


def back_kernel(
    lat_ref,
    gain_ref,
    grad_ref,
    next_ref,
    low_ref,
    high_ref,
    own_ref,
    oth_ref,
    out_ref,
    sums_ref,
    ext,
    acc,
):
    step = pl.program_id(0)

    @pl.when(step == 0)
    def _():
        me = lax.axis_index("dp")
        for f in range(4):
            for r in range(4):
                if r == 0:
                    block = low_ref[f]
                elif r == 3:
                    block = high_ref[f]
                elif f < 2:
                    block = grad_ref[f, r - 1]
                else:
                    block = next_ref[f - 2, r - 1]
                for s, shifted in enumerate(shifted_columns(block)):
                    first, second = shifted[:, :HALF], shifted[:, HALF:]
                    ext[0, s, f, r] = jnp.where(me == 0, first, second)
                    ext[1, s, f, r] = jnp.where(me == 0, second, first)
        acc[...] = jnp.zeros_like(acc)

    tap_t, tap_h = step // 3, step % 3
    windows = []
    weights = []
    for half, ref in enumerate((own_ref, oth_ref)):
        for c in range(3):
            windows.append(
                ext[half, 2 - c, pl.ds(2 - tap_t, 2), pl.ds(2 - tap_h, 2)].reshape(CELLS, HALF)
            )
            weights.append(ref[pl.ds(CH * c, CH), :])
    acc[...] += lax.dot_general(
        jnp.concatenate(windows, axis=-1),
        jnp.concatenate(weights, axis=-1),
        (((1,), (1,)), ((), ())),
        preferred_element_type=F32,
    )

    @pl.when(step == 8)
    def _():
        gain_sum = jnp.zeros((1, CH), F32)
        bias_sum = jnp.zeros((1, CH), F32)
        gain = gain_ref[...]
        for j in range(4):
            rows = pl.ds(COLS * j, COLS)
            floats = lat_ref[rows, :].astype(F32)
            scale, normed = normalised(floats)
            pre_act = normed * gain
            sig = 1.0 / (1.0 + jnp.exp(-pre_act))
            pre_grad = acc[rows, :] * sig * (1.0 + pre_act * (1.0 - sig))
            grads = grad_ref[j // 2, j % 2].astype(F32)
            gain_sum += jnp.sum(pre_grad * normed, axis=0, keepdims=True)
            bias_sum += jnp.sum(grads, axis=0, keepdims=True)
            normed_grad = pre_grad * gain
            along = jnp.mean(normed_grad * normed, axis=-1, keepdims=True)
            out_ref[rows, :] = (grads + scale * (normed_grad - normed * along)).astype(BF16)
        for part in range(4):
            sums_ref[pl.ds(part, 1), :] = gain_sum[:, 128 * part : 128 * part + 128]
            sums_ref[pl.ds(4 + part, 1), :] = bias_sum[:, 128 * part : 128 * part + 128]


def weight_kernel(mix_ref, halo_ref, sums_ref, keep_ref, send_ref, acts, grads, acc):
    grad_scale = 1.0 / (TOTAL**0.5)
    zero = jnp.zeros((10, COLS, 128), BF16)
    grads[:, pl.ds(0, 1)] = zero.reshape(10, 1, COLS, 128)
    grads[:, pl.ds(9, 1)] = zero.reshape(10, 1, COLS, 128)
    for y in range(4):
        for x in range(4):
            for f in range(2):
                for r in range(2):
                    row = 2 * x + r
                    grads[2 * y + f, 1 + row] = mix_ref[4 * y + x, 1, f, r]
                    block = mix_ref[4 * y + x, 0, f, r]
                    for c, shifted in enumerate(shifted_columns(block)):
                        acts[y, c, pl.ds(640 * f + COLS * row, COLS), :] = shifted
    for x in range(4):
        for f in range(2):
            for r in range(2):
                grads[8 + f, 1 + 2 * x + r] = halo_ref[x, f, r]
    acc[...] = jnp.zeros_like(acc)

    @pl.loop(0, 4)
    def _(pair):
        left = jnp.concatenate([acts[pair, c] for c in range(3)], axis=-1)
        right = jnp.concatenate(
            [
                grads[pl.ds(2 * pair + 2 - a, 2), pl.ds(2 - b, 8)].reshape(1280, 128)
                for a in range(3)
                for b in range(3)
            ],
            axis=-1,
        )
        acc[...] += lax.dot_general(
            left, right, (((0,), (0,)), ((), ())), preferred_element_type=F32
        )

    me = lax.axis_index("dp")
    for ab in range(9):
        for c in range(3):
            block = acc[pl.ds(128 * c, 128), pl.ds(128 * ab, 128)] * grad_scale
            top, bottom = block[:64], block[64:]
            first = jnp.concatenate([top[:, :64], bottom[:, :64]], axis=-1)
            second = jnp.concatenate([top[:, 64:], bottom[:, 64:]], axis=-1)
            rows = pl.ds(64 * (3 * ab + c), 64)
            keep_ref[rows, :] = jnp.where(me == 0, first, second)
            send_ref[rows, :] = jnp.where(me == 0, second, first)
    keep_ref[pl.ds(1728, 8), :] = sums_ref[...] * grad_scale
    send_ref[pl.ds(1728, 8), :] = sums_ref[...] * grad_scale


def first_tap(z, x):
    return jnp.minimum(lax.div(lax.div(27 * z - x + 3, 4), 2), 23)


def split_kernel(keep_ref, got_ref, piece_ref, mine_ref, both):
    both[...] = keep_ref[...] + got_ref[...]
    z, x = lax.axis_index("z"), lax.axis_index("x")
    total = both[pl.ds(1728, 8), :]
    high = total.astype(BF16).astype(F32)
    mid = (total - high).astype(BF16).astype(F32)
    low = total - high - mid
    terms = jnp.concatenate([high, mid, low, jnp.zeros_like(low)], axis=0).astype(BF16)
    for k in range(8):
        target = lax.rem(z + k, 8)
        start = pl.multiple_of(64 * first_tap(target, x), 64)
        if k == 0:
            mine_ref[pl.ds(0, 256), :] = both[pl.ds(start, 256), :]
            mine_ref[pl.ds(256, 8), :] = total
        else:
            piece_ref[k - 1, pl.ds(0, 256), :] = both[pl.ds(start, 256), :].astype(BF16)
            piece_ref[k - 1, pl.ds(256, 32), :] = terms


def sum_kernel(mine_ref, *refs):
    got_refs, out_ref, taps = refs[:7], refs[7], refs[8]
    z, x = lax.axis_index("z"), lax.axis_index("x")
    block = mine_ref[pl.ds(0, 256), :]
    total = mine_ref[pl.ds(256, 8), :]
    for got in got_refs:
        block += got[pl.ds(0, 256), :].astype(F32)
        terms = got[pl.ds(256, 32), :].astype(F32)
        total += terms[0:8] + terms[8:16] + terms[16:24]
    taps[...] = block
    lane = lax.broadcasted_iota(jnp.int32, (64, 128), 1)
    for y in range(4):
        group = lax.div(27 * (4 * z + y), 4)
        unit = lax.div(group - x + 3, 4)
        tap = lax.div(unit, 2) - first_tap(z, x)
        odd = lax.rem(unit, 2)
        here = taps[pl.ds(pl.multiple_of(64 * jnp.minimum(tap, 3), 64), 64), :]
        after = taps[pl.ds(pl.multiple_of(64 * jnp.minimum(tap + 1, 3), 64), 64), :]
        crossed = pltpu.roll(jnp.where(lane >= 64, here, after), 64, 1)
        piece = jnp.where(odd == 1, crossed, here)
        for other in range(4):
            out_ref[4 * y + other, pl.ds(0, 64), :] = piece
            out_ref[4 * y + other, pl.ds(64, 8), :] = total


def final_kernel(got_ref, out_ref, sums_ref, rows):
    z, y = lax.axis_index("z"), lax.axis_index("y")
    index = 4 * z + y
    group = lax.div(27 * index, 4)
    for j in range(8):
        source = lax.rem(group + j, 4)
        pieces = []
        for part in range(4):
            block = got_ref[4 * part + source, pl.ds(0, 64), :]
            pieces.append(block[:, :64] if j < 4 else block[:, 64:])
        rows[pl.ds(64 * j, 64), :] = jnp.concatenate(pieces, axis=-1)
    offset = pl.multiple_of(16 * lax.rem(27 * index, 4), 16)
    out_ref[...] = rows[pl.ds(offset, 432), :]
    total = got_ref[0, pl.ds(64, 8), :]
    for k in range(1, 16):
        total += got_ref[k, pl.ds(64, 8), :]
    sums_ref[...] = total


def shape(dims, dtype):
    return jax.ShapeDtypeStruct(dims, dtype)


def moved(block, axis, distance):
    count = AXES[axis]
    return lax.ppermute(block, axis, [(i, (i + distance) % count) for i in range(count)])


def neighbour(block, axes, count, distance):
    route = [(i, i + distance) for i in range(count) if 0 <= i + distance < count]
    return lax.ppermute(block, axes, route)


def whole(dims):
    return pl.BlockSpec(dims, lambda i: (0,) * len(dims))


def on_device(latents, norm_gain, kernel, conv_bias, out_grad):
    lat_flat = latents.reshape(CELLS, CH)
    gain_row = norm_gain.reshape(1, CH)
    bias_row = conv_bias.reshape(1, CH)
    grad = out_grad.reshape(2, 2, COLS, CH)

    kernel_other = moved(kernel, "dp", 1)
    later = neighbour(grad, ("z", "y"), 32, -1)

    act_flat, mix = pl.pallas_call(
        act_kernel,
        out_shape=(shape((CELLS, CH), BF16), shape((16, 2, CELLS, 128), BF16)),
        compiler_params=BIG,
        name="act",
    )(lat_flat, gain_row, grad.reshape(CELLS, CH))
    act = act_flat.reshape(2, 2, COLS, CH)
    earlier = neighbour(act, ("z", "y"), 32, 1)

    mixed = lax.all_to_all(mix, ("y", "x"), 0, 0).reshape(16, 2, 2, 2, COLS, 128)
    halo = neighbour(mixed[0:4, 1], "z", 8, -1)

    frames_grad = jnp.concatenate([grad, later], axis=0)
    frames_act = jnp.concatenate([earlier, act], axis=0)
    edge_up = jnp.stack([frames_grad[:, 1], frames_act[:, 1]])
    edge_down = jnp.stack([frames_grad[:, 0], frames_act[:, 0]])
    low = neighbour(edge_up, "x", 4, 1)
    high = neighbour(edge_down, "x", 4, -1)

    weight_specs = [pl.BlockSpec((3 * CH, HALF), lambda i: (i, 0))] * 2
    tile = (2, 2, COLS, CH)
    edge = (4, COLS, CH)
    latent_grad, sums = pl.pallas_call(
        back_kernel,
        grid=(9,),
        in_specs=[whole((CELLS, CH)), whole((1, CH)), whole(tile), whole(tile)]
        + [whole(edge), whole(edge)]
        + weight_specs,
        out_specs=(whole((CELLS, CH)), whole((8, 128))),
        out_shape=(shape((CELLS, CH), BF16), shape((8, 128), F32)),
        scratch_shapes=[
            pltpu.VMEM((2, 3, 4, 4, COLS, HALF), BF16),
            pltpu.VMEM((CELLS, CH), F32),
        ],
        compiler_params=BIG,
        cost_estimate=pl.CostEstimate(
            flops=2 * CELLS * 27 * CH * CH, bytes_accessed=16_000_000, transcendentals=0
        ),
        name="back",
    )(lat_flat, gain_row, grad, later, low[0], high[0], kernel, kernel_other)

    block_out = pl.pallas_call(
        conv_kernel,
        grid=(9,),
        in_specs=[whole((CELLS, CH)), whole((1, CH)), whole(tile), whole(tile)]
        + [whole(edge), whole(edge)]
        + weight_specs,
        out_specs=whole((CELLS, CH)),
        out_shape=shape((CELLS, CH), BF16),
        scratch_shapes=[
            pltpu.VMEM((3, 4, 4, COLS, CH), BF16),
            pltpu.VMEM((2, CELLS, HALF), F32),
        ],
        compiler_params=BIG,
        cost_estimate=pl.CostEstimate(
            flops=2 * CELLS * 27 * CH * CH, bytes_accessed=16_000_000, transcendentals=0
        ),
        name="conv",
    )(lat_flat, bias_row, act, earlier, low[1], high[1], kernel, kernel_other)

    keep, send = pl.pallas_call(
        weight_kernel,
        out_shape=(shape((1736, 128), F32), shape((1736, 128), F32)),
        scratch_shapes=[
            pltpu.VMEM((4, 3, 1280, 128), BF16),
            pltpu.VMEM((10, 10, COLS, 128), BF16),
            pltpu.VMEM((384, 1152), F32),
        ],
        compiler_params=BIG,
        cost_estimate=pl.CostEstimate(
            flops=2 * CELLS * 27 * CH * CH, bytes_accessed=5_000_000, transcendentals=0
        ),
        name="weight",
    )(mixed, halo, sums)
    got = moved(send, "dp", 1)

    pieces, mine = pl.pallas_call(
        split_kernel,
        out_shape=(shape((7, 288, 128), BF16), shape((264, 128), F32)),
        scratch_shapes=[pltpu.VMEM((1736, 128), F32)],
        compiler_params=BIG,
        name="split",
    )(keep, got)
    arrived = [moved(pieces[k - 1], "z", k) for k in range(1, 8)]
    spread = pl.pallas_call(
        sum_kernel,
        out_shape=shape((16, 72, 128), F32),
        scratch_shapes=[pltpu.VMEM((256, 128), F32)],
        compiler_params=BIG,
        name="sum",
    )(mine, *arrived)
    gathered = lax.all_to_all(spread, ("y", "x"), 0, 0)
    kernel_grad, totals = pl.pallas_call(
        final_kernel,
        out_shape=(shape((432, 256), F32), shape((8, 128), F32)),
        scratch_shapes=[pltpu.VMEM((512, 256), F32)],
        compiler_params=BIG,
        name="final",
    )(gathered)
    return (
        block_out.reshape(latents.shape),
        latent_grad.reshape(latents.shape),
        kernel_grad,
        totals[:4].reshape(CH),
        totals[4:].reshape(CH),
    )


def solution(mesh):
    fine = Mesh(mesh.devices.reshape(2, 8, 4, 4), ("dp", "z", "y", "x"))
    cells = P("dp", ("z", "y"), "x", None, None)
    return jax.shard_map(
        on_device,
        mesh=fine,
        in_specs=(cells, P(), P(None, "dp"), P(), cells),
        out_specs=(cells, cells, P(("z", "y"), "dp"), P(), P()),
        check_vma=False,
    )
```

time: 443 us -> 166 us (0.37)
  waiting for transfers between devices: 259 us -> 53.3 us
  blocking collectives: 84.9 us -> 0 us
  Pallas kernels: 0 us -> 46.2 us
  starting transfers between devices: 19.9 us -> 52.9 us
  matrix products: 25.3 us -> 0 us
  local copies, waits for them, and re-layouts: 29.6 us -> 11.4 us
  between operations: 14.4 us -> 0.84 us
  other arithmetic: 7.21 us -> 0.18 us
    reduce_scatter x2 -> x0, waiting for transfers between devices: 185 us -> none  [the longest x1 166 us: on_device(): lax.psum_scatter(kernel_local, 'tm', scatter_dimension=0, tiled=True)]
    psum x1 -> x0, blocking collectives: 76.5 us -> none  [on_device(): lax.psum((gain_local, bias_local), ('dp', 'tm', 'space'))]
    pallas_call x0 -> x7, Pallas kernels: none -> 46.2 us  [the longest x1 13.4 us: on_device(): pl.pallas_call(back_kernel, grid=(9,), in_specs=[whole((CELLS, CH)), whol...]
    psum x1 -> x0, waiting for transfers between devices: 32.3 us -> none  [on_device(): kernel_grad = lax.psum(row_part, 'space')]
    ppermute x6 -> x14, waiting for transfers between devices: 25.7 us -> 53.3 us  [the longest x5 42.3 us: neighbour(): return lax.ppermute(block, axes, route)]
    dot_general x3 -> x0, matrix products: 25.3 us -> none  [the longest x1 10.5 us: on_device(): conv_part = jnp.dot(act_taps, kernel, preferred_element_type=jnp.float32)]
    all_to_all x0 -> x2, starting transfers between devices: none -> 18.5 us  [the longest x1 10.9 us: on_device(): gathered = lax.all_to_all(spread, ('y', 'x'), 0, 0)]
    all_gather x1 -> x0, waiting for transfers between devices: 16.3 us -> none  [on_device(): act_pair = lax.all_gather(act_ext, 'dp', axis=0, tiled=True)]
  transfers between devices with their start and end apart: 10 -> 16, of which waited for: 8 -> 9; matrix products, arithmetic and copies ran while one was open for 5% -> 2% of each run, Pallas kernels for 0% -> 18%
where the time goes in v1:
time: 166 us; the launch traced here: 165 us
  waiting for transfers between devices  53.3 us (32%)
  starting transfers between devices  52.9 us (32%)
  Pallas kernels  46.2 us (28%)
  local copies, waits for them, and re-layouts  11.4 us (7%)
    ppermute x5, waiting for transfers between devices, neighbour(): return lax.ppermute(block, axes, route)  42.3 us
    ppermute x9, starting transfers between devices, moved(): lax.ppermute(block, axis, [(i, (i + distance) % count) for i in range(cou...  18.6 us
    ppermute x5, starting transfers between devices, neighbour(): return lax.ppermute(block, axes, route)  15.8 us
    pallas_call x1, Pallas kernels, on_device(): pl.pallas_call(back_kernel, grid=(9,), in_specs=[whole((CELLS, CH)), whol...  13.4 us
    pallas_call x1, Pallas kernels, on_device(): pl.pallas_call(conv_kernel, grid=(9,), in_specs=[whole((CELLS, CH)), whol...  12.4 us
    ppermute x9, waiting for transfers between devices, moved(): lax.ppermute(block, axis, [(i, (i + distance) % count) for i in range(cou...  11 us
    all_to_all x1, starting transfers between devices, on_device(): gathered = lax.all_to_all(spread, ('y', 'x'), 0, 0)  10.9 us
    pallas_call x1, Pallas kernels, on_device(): pl.pallas_call(weight_kernel, out_shape=(shape((1736, 128), F32), shape((...  10.4 us
  transfers between devices with their start and end apart: 16, of which 9 were waited for; matrix products, arithmetic and copies ran while one was open for 2% of the time, Pallas kernels for 18%

profile of v1, /device:TPU:34, one launch (start us, length us, event | category | flops | bytes accessed | tf_op | source)
XLA Modules:
  0.0 164.8 jit_solution(26139281054537791)
XLA Ops:
  0.6 0.1 collective-permute-start.4
  0.7 3.4 %act.1 = (bf16[320,512]{1,0:T(8,128)(2,1)}, bf16[16,2,320,128]{3,2,1,0:T(8,128)(2,1)}) custom-call(bf16[320,512]{1,0:T(8,128)(2,1)} %bitcast.58, f32[1,512]{1,0:T(1,128)} %bitcast.61, bf16[320,512]{1,0:T(8,128)(2,1)} %bitcast.53), custom_call_target="tpu_custom_call" | custom-call | tf_op jit(solution)/shard_map/act/pallas_call | solution.py:313
  4.1 7.6 %all-to-all-start = ((bf16[16,2,320,128]{3,2,1,0:T(8,128)(2,1)}), bf16[16,2,320,128]{3,2,1,0:T(8,128)(2,1)S(1)}, u32[]{:S(2)}, u32[]{:S(2)}) async-start(bf16[16,2,320,128]{3,2,1,0:T(8,128)(2,1)} %get-tuple-element.17), calls=%async_computation | async-start | bytes 5242880 | tf_op jit(solution)/shard_map/all_to_all | solution.py:322
  11.7 0.0 copy-done.3
  11.7 3.4 %collective-permute-start = (bf16[2,2,80,512]{3,2,0,1:T(8,128)(2,1)S(1)}, bf16[2,2,80,512]{3,2,0,1:T(8,128)(2,1)S(1)}, u32[]{:S(2)}, u32[]{:S(2)}) collective-permute-start(bf16[2,2,80,512]{3,2,0,1:T(8,128)(2,1)S(1)} %copy.17), channel_id=1, source_target_pairs={{0,4},{4,8},{8,12},{12,16},{16,20},{20,24},{24,28},{28,32},{32,36}... | collective-permute-start | bytes 983048 | tf_op jit(solution)/shard_map/ppermute | solution.py:297
  15.1 0.0 copy-done.2
  15.2 4.6 %collective-permute-start.1 = (bf16[2,2,80,512]{3,2,0,1:T(8,128)(2,1)S(1)}, bf16[2,2,80,512]{3,2,0,1:T(8,128)(2,1)S(1)}, u32[]{:S(2)}, u32[]{:S(2)}) collective-permute-start(bf16[2,2,80,512]{3,2,0,1:T(8,128)(2,1)S(1)} %bitcast.51), channel_id=1, source_target_pairs={{4,0},{8,4},{12,8},{16,12},{20,16},{24,20},{28,24},{32,28},{36,32}... | collective-permute-start | bytes 983048 | tf_op jit(solution)/shard_map/ppermute | solution.py:297
  19.7 24.1 %collective-permute-done = bf16[2,2,80,512]{3,2,0,1:T(8,128)(2,1)S(1)} collective-permute-done((bf16[2,2,80,512]{3,2,0,1:T(8,128)(2,1)S(1)}, bf16[2,2,80,512]{3,2,0,1:T(8,128)(2,1)S(1)}, u32[]{:S(2)}, u32[]{:S(2)}) %collective-permute-start) | collective-permute-done | bytes 327712 | tf_op jit(solution)/shard_map/ppermute | solution.py:297
  43.9 0.7 copy-done.4
  44.6 5.5 %collective-permute-done.1 = bf16[2,2,80,512]{3,2,0,1:T(8,128)(2,1)S(1)} collective-permute-done((bf16[2,2,80,512]{3,2,0,1:T(8,128)(2,1)S(1)}, bf16[2,2,80,512]{3,2,0,1:T(8,128)(2,1)S(1)}, u32[]{:S(2)}, u32[]{:S(2)}) %collective-permute-start.1) | collective-permute-done | bytes 327712 | tf_op jit(solution)/shard_map/ppermute | solution.py:297
  50.1 0.1 fusion.2
  50.2 0.1 pad_maximum_fusion
  50.3 2.6 %collective-permute-start.2 = (bf16[2,4,80,512]{3,2,1,0:T(8,128)(2,1)S(1)}, bf16[2,4,80,512]{3,2,1,0:T(8,128)(2,1)S(1)}, u32[]{:S(2)}, u32[]{:S(2)}) collective-permute-start(bf16[2,4,80,512]{3,2,1,0:T(8,128)(2,1)S(1)} %pad_maximum_fusion), channel_id=1, source_target_pairs={{0,1},{1,2},{2,3},{4,5},{5,6},{6,7},{8,9},{9,10},{10,11},{12,13},{... | collective-permute-start | bytes 1966088 | tf_op jit(solution)/shard_map/ppermute | solution.py:297
  52.9 0.1 pad_maximum_fusion.1
  53.0 3.3 %collective-permute-start.3 = (bf16[2,4,80,512]{3,2,1,0:T(8,128)(2,1)S(1)}, bf16[2,4,80,512]{3,2,1,0:T(8,128)(2,1)S(1)}, u32[]{:S(2)}, u32[]{:S(2)}) collective-permute-start(bf16[2,4,80,512]{3,2,1,0:T(8,128)(2,1)S(1)} %pad_maximum_fusion.1), channel_id=1, source_target_pairs={{1,0},{2,1},{3,2},{5,4},{6,5},{7,6},{9,8},{10,9},{11,10},{13,12},{... | collective-permute-start | bytes 1966088 | tf_op jit(solution)/shard_map/ppermute | solution.py:297
  56.3 0.8 copy.22.next_ref
  57.0 11.2 %collective-permute-done.2 = bf16[2,4,80,512]{3,2,1,0:T(8,128)(2,1)S(1)} collective-permute-done((bf16[2,4,80,512]{3,2,1,0:T(8,128)(2,1)S(1)}, bf16[2,4,80,512]{3,2,1,0:T(8,128)(2,1)S(1)}, u32[]{:S(2)}, u32[]{:S(2)}) %collective-permute-start.2) | collective-permute-done | bytes 655392 | tf_op jit(solution)/shard_map/ppermute | solution.py:297
  68.2 0.9 slice_bitcast_fusion.2
  69.1 1.5 collective-permute-done.3
  70.6 0.9 slice_bitcast_fusion.1
  71.5 0.0 all-to-all-done
  71.5 0.2 copy.23
  71.7 1.4 copy-done
  73.1 2.0 %collective-permute-start.5 = (bf16[4,2,2,80,128]{4,3,2,1,0:T(8,128)(2,1)S(1)}, bf16[4,2,2,80,128]{4,3,2,1,0:T(8,128)(2,1)S(1)}, u32[]{:S(2)}, u32[]{:S(2)}) collective-permute-start(bf16[4,2,2,80,128]{4,3,2,1,0:T(8,128)(2,1)S(1)} %slice_bitcast_fusion), channel_id=1, source_target_pairs={{16,0},{32,16},{48,32},{64,48},{80,64},{96,80},{112,96},{17,1},{33... | collective-permute-start | bytes 983048 | tf_op jit(solution)/shard_map/ppermute | solution.py:297
  75.1 0.0 collective-permute-done.4.oth_ref
  75.1 13.4 %back.1 = (bf16[320,512]{1,0:T(8,128)(2,1)}, f32[8,128]{1,0:T(8,128)}) custom-call(bf16[320,512]{1,0:T(8,128)(2,1)} %bitcast.59, f32[1,512]{1,0:T(1,128)} %bitcast.62, bf16[2,2,80,512]{3,2,1,0:T(8,128)(2,1)} %bitcast.54, bf16[2,2,80,512]{3,2,1,0:T(8,128)(2,1)} %copy.22.next_ref, bf16[4,80,512]{2,1,0:T(8,128)(2,1)} %get-tuple-element.27.low_ref, ...), custom_call_target="tpu_custom_call" | custom-call | flops 4529848320 | bytes 16000000 | tf_op jit(solution)/shard_map/back/pallas_call | solution.py:335
  88.5 0.0 collective-permute-done.5.halo_ref
  88.5 0.0 copy-start.14
  88.5 0.7 copy-done.14
  89.2 10.4 %weight.1 = (f32[1736,128]{1,0:T(8,128)}, f32[1736,128]{1,0:T(8,128)}) custom-call(bf16[16,2,2,2,80,128]{5,4,3,2,1,0:T(8,128)(2,1)} %bitcast.49, bf16[4,2,2,80,128]{4,3,2,1,0:T(8,128)(2,1)} %copy-done.14, f32[8,128]{1,0:T(8,128)} %get-tuple-element.18.sums_ref), custom_call_target="tpu_custom_call" | custom-call | flops 4529848320 | bytes 5000000 | tf_op jit(solution)/shard_map/weight/pallas_call | solution.py:373
  99.6 0.0 collective-permute-start.6
  99.6 2.6 %collective-permute-done.6.got_ref = f32[1736,128]{1,0:T(8,128)S(1)} collective-permute-done((f32[1736,128]{1,0:T(8,128)}, f32[1736,128]{1,0:T(8,128)S(1)}, u32[]{:S(2)}, u32[]{:S(2)}) %collective-permute-start.6) | collective-permute-done | bytes 888864 | tf_op jit(solution)/shard_map/ppermute | solution.py:292
  102.3 1.0 copy-done.6
  103.3 2.5 %split.1 = (bf16[7,288,128]{2,1,0:T(8,128)(2,1)}, f32[264,128]{1,0:T(8,128)}) custom-call(f32[1736,128]{1,0:T(8,128)} %get-tuple-element.19.keep_ref, f32[1736,128]{1,0:T(8,128)} %copy-done.6), custom_call_target="tpu_custom_call" | custom-call | tf_op jit(solution)/shard_map/split/pallas_call | solution.py:389
  105.8 1.1 slice_bitcast_fusion.7
  106.9 2.0 %collective-permute-start.7 = (bf16[288,128]{1,0:T(8,128)(2,1)S(1)}, bf16[288,128]{1,0:T(8,128)(2,1)S(1)}, u32[]{:S(2)}, u32[]{:S(2)}) collective-permute-start(bf16[288,128]{1,0:T(8,128)(2,1)S(1)} %get-tuple-element.39), channel_id=1, source_target_pairs={{0,16},{16,32},{32,48},{48,64},{64,80},{80,96},{96,112},{112,0},{1... | collective-permute-start | bytes 221192 | tf_op jit(solution)/shard_map/ppermute | solution.py:292
  108.9 4.5 %collective-permute-start.8 = (bf16[288,128]{1,0:T(8,128)(2,1)S(1)}, bf16[288,128]{1,0:T(8,128)(2,1)S(1)}, u32[]{:S(2)}, u32[]{:S(2)}) collective-permute-start(bf16[288,128]{1,0:T(8,128)(2,1)S(1)} %get-tuple-element.38), channel_id=1, source_target_pairs={{0,32},{16,48},{32,64},{48,80},{64,96},{80,112},{96,0},{112,16},{1... | collective-permute-start | bytes 221192 | tf_op jit(solution)/shard_map/ppermute | solution.py:292
  113.4 2.9 %collective-permute-start.9 = (bf16[288,128]{1,0:T(8,128)(2,1)S(1)}, bf16[288,128]{1,0:T(8,128)(2,1)S(1)}, u32[]{:S(2)}, u32[]{:S(2)}) collective-permute-start(bf16[288,128]{1,0:T(8,128)(2,1)S(1)} %get-tuple-element.37), channel_id=1, source_target_pairs={{0,48},{16,64},{32,80},{48,96},{64,112},{80,0},{96,16},{112,32},{1... | collective-permute-start | bytes 221192 | tf_op jit(solution)/shard_map/ppermute | solution.py:292
  116.3 0.5 collective-permute-start.10
  116.8 4.1 %collective-permute-start.11 = (bf16[288,128]{1,0:T(8,128)(2,1)S(1)}, bf16[288,128]{1,0:T(8,128)(2,1)S(1)}, u32[]{:S(2)}, u32[]{:S(2)}) collective-permute-start(bf16[288,128]{1,0:T(8,128)(2,1)S(1)} %get-tuple-element.35), channel_id=1, source_target_pairs={{0,80},{16,96},{32,112},{48,0},{64,16},{80,32},{96,48},{112,64},{1... | collective-permute-start | bytes 221192 | tf_op jit(solution)/shard_map/ppermute | solution.py:292
  120.8 0.0 collective-permute-done.7.refs_0_
  120.8 2.4 %collective-permute-start.12 = (bf16[288,128]{1,0:T(8,128)(2,1)S(1)}, bf16[288,128]{1,0:T(8,128)(2,1)S(1)}, u32[]{:S(2)}, u32[]{:S(2)}) collective-permute-start(bf16[288,128]{1,0:T(8,128)(2,1)S(1)} %get-tuple-element.34), channel_id=1, source_target_pairs={{0,96},{16,112},{32,0},{48,16},{64,32},{80,48},{96,64},{112,80},{1... | collective-permute-start | bytes 221192 | tf_op jit(solution)/shard_map/ppermute | solution.py:292
  123.2 0.0 collective-permute-done.8.refs_1_
  123.2 2.2 %collective-permute-start.13 = (bf16[288,128]{1,0:T(8,128)(2,1)S(1)}, bf16[288,128]{1,0:T(8,128)(2,1)S(1)}, u32[]{:S(2)}, u32[]{:S(2)}) collective-permute-start(bf16[288,128]{1,0:T(8,128)(2,1)S(1)} %get-tuple-element.33), channel_id=1, source_target_pairs={{0,112},{16,0},{32,16},{48,32},{64,48},{80,64},{96,80},{112,96},{1... | collective-permute-start | bytes 221192 | tf_op jit(solution)/shard_map/ppermute | solution.py:292
  125.4 1.9 %collective-permute-done.9.refs_2_ = bf16[288,128]{1,0:T(8,128)(2,1)S(1)} collective-permute-done((bf16[288,128]{1,0:T(8,128)(2,1)S(1)}, bf16[288,128]{1,0:T(8,128)(2,1)S(1)}, u32[]{:S(2)}, u32[]{:S(2)}) %collective-permute-start.9) | collective-permute-done | bytes 73760 | tf_op jit(solution)/shard_map/ppermute | solution.py:292
  127.4 0.0 collective-permute-done.10.refs_3_
  127.4 1.9 %collective-permute-done.11.refs_4_ = bf16[288,128]{1,0:T(8,128)(2,1)S(1)} collective-permute-done((bf16[288,128]{1,0:T(8,128)(2,1)S(1)}, bf16[288,128]{1,0:T(8,128)(2,1)S(1)}, u32[]{:S(2)}, u32[]{:S(2)}) %collective-permute-start.11) | collective-permute-done | bytes 73760 | tf_op jit(solution)/shard_map/ppermute | solution.py:292
  129.3 3.7 %collective-permute-done.12.refs_5_ = bf16[288,128]{1,0:T(8,128)(2,1)S(1)} collective-permute-done((bf16[288,128]{1,0:T(8,128)(2,1)S(1)}, bf16[288,128]{1,0:T(8,128)(2,1)S(1)}, u32[]{:S(2)}, u32[]{:S(2)}) %collective-permute-start.12) | collective-permute-done | bytes 73760 | tf_op jit(solution)/shard_map/ppermute | solution.py:292
  133.0 0.8 collective-permute-done.13.refs_6_
  133.8 0.0 copy-done.7
  133.8 0.0 copy-done.8
  133.8 0.0 copy-done.9
  133.8 0.0 copy-done.10
  133.8 0.0 copy-done.11
  133.8 0.0 copy-done.12
  133.8 0.6 copy-done.13
  134.4 2.2 %sum.1 = f32[16,72,128]{2,1,0:T(8,128)} custom-call(f32[264,128]{1,0:T(8,128)} %get-tuple-element.21.mine_ref, bf16[288,128]{1,0:T(8,128)(2,1)} %copy-done.7, bf16[288,128]{1,0:T(8,128)(2,1)} %copy-done.8, bf16[288,128]{1,0:T(8,128)(2,1)} %copy-done.9, bf16[288,128]{1,0:T(8,128)(2,1)} %copy-done.10, bf16[288,128]{1,0:T(8,128)(2,1)} %copy-done.11, ...), custom_call_target="tpu_custom_call" | custom-call | tf_op jit(solution)/shard_map/sum/pallas_call | solution.py:397
  136.6 10.9 %all-to-all-start.1 = ((f32[16,72,128]{2,1,0:T(8,128)}), f32[16,72,128]{2,1,0:T(8,128)S(1)}, u32[]{:S(2)}, u32[]{:S(2)}) async-start(f32[16,72,128]{2,1,0:T(8,128)} %sum.1), calls=%async_computation.1 | async-start | bytes 1179648 | tf_op jit(solution)/shard_map/all_to_all | solution.py:404
  147.5 0.8 copy.20.prev_ref
  148.2 12.4 %conv.1 = bf16[320,512]{1,0:T(8,128)(2,1)} custom-call(bf16[320,512]{1,0:T(8,128)(2,1)} %bitcast.60, f32[1,512]{1,0:T(1,128)} %bitcast.63, bf16[2,2,80,512]{3,2,1,0:T(8,128)(2,1)} %bitcast.55, bf16[2,2,80,512]{3,2,1,0:T(8,128)(2,1)} %copy.20.prev_ref, bf16[4,80,512]{2,1,0:T(8,128)(2,1)} %get-tuple-element.28.low_ref, ...), custom_call_target="tpu_custom_call" | custom-call | flops 4529848320 | bytes 16000000 | tf_op jit(solution)/shard_map/conv/pallas_call | solution.py:354
  160.6 0.0 all-to-all-done.1.got_ref
  160.6 0.8 copy-done.1
  161.4 2.1 %final.1 = (f32[432,256]{1,0:T(8,128)}, f32[8,128]{1,0:T(8,128)}) custom-call(f32[16,72,128]{2,1,0:T(8,128)} %copy-done.1), custom_call_target="tpu_custom_call" | custom-call | tf_op jit(solution)/shard_map/final/pallas_call | solution.py:405
  163.5 1.3 slice_bitcast_fusion.14
  (21 shorter events, 0.2 us)
Async XLA Ops:
  0.6 74.5 %collective-permute-start.4 = (bf16[13824,256]{1,0:T(8,128)(2,1)}, bf16[13824,256]{1,0:T(8,128)(2,1)}, u32[]{:S(2)}, u32[]{:S(2)}) collective-permute-start(bf16[13824,256]{1,0:T(8,128)(2,1)} %own_ref.3), channel_id=1, source_target_pairs={{0,128},{128,0},{1,129},{129,1},{2,130},{130,2},{3,131},{131,3},{4... | collective-permute-start | bytes 21233672 | tf_op jit(solution)/shard_map/ppermute | solution.py:292
  4.1 7.6 %copy-start.3 = (bf16[320,512]{1,0:T(8,128)(2,1)S(1)}, bf16[320,512]{1,0:T(8,128)(2,1)}, u32[]{:S(2)}) copy-start(bf16[320,512]{1,0:T(8,128)(2,1)} %get-tuple-element.15) | copy-start | bytes 983044
  4.1 11.0 %copy-start.2 = (bf16[1,2,2,80,512]{4,3,2,1,0:T(8,128)(2,1)S(1)}, bf16[1,2,2,80,512]{4,3,2,1,0:T(8,128)(2,1)}, u32[]{:S(2)}) copy-start(bf16[1,2,2,80,512]{4,3,2,1,0:T(8,128)(2,1)} %param.9) | copy-start | bytes 983044
  4.1 67.4 %all-to-all-start = ((bf16[16,2,320,128]{3,2,1,0:T(8,128)(2,1)}), bf16[16,2,320,128]{3,2,1,0:T(8,128)(2,1)S(1)}, u32[]{:S(2)}, u32[]{:S(2)}) async-start(bf16[16,2,320,128]{3,2,1,0:T(8,128)(2,1)} %get-tuple-element.17), calls=%async_computation | async-start | bytes 5242880 | tf_op jit(solution)/shard_map/all_to_all | solution.py:322
  11.7 32.1 %collective-permute-start = (bf16[2,2,80,512]{3,2,0,1:T(8,128)(2,1)S(1)}, bf16[2,2,80,512]{3,2,0,1:T(8,128)(2,1)S(1)}, u32[]{:S(2)}, u32[]{:S(2)}) collective-permute-start(bf16[2,2,80,512]{3,2,0,1:T(8,128)(2,1)S(1)} %copy.17), channel_id=1, source_target_pairs={{0,4},{4,8},{8,12},{12,16},{16,20},{20,24},{24,28},{28,32},{32,36}... | collective-permute-start | bytes 983048 | tf_op jit(solution)/shard_map/ppermute | solution.py:297
  15.2 34.9 %collective-permute-start.1 = (bf16[2,2,80,512]{3,2,0,1:T(8,128)(2,1)S(1)}, bf16[2,2,80,512]{3,2,0,1:T(8,128)(2,1)S(1)}, u32[]{:S(2)}, u32[]{:S(2)}) collective-permute-start(bf16[2,2,80,512]{3,2,0,1:T(8,128)(2,1)S(1)} %bitcast.51), channel_id=1, source_target_pairs={{4,0},{8,4},{12,8},{16,12},{20,16},{24,20},{28,24},{32,28},{36,32}... | collective-permute-start | bytes 983048 | tf_op jit(solution)/shard_map/ppermute | solution.py:297
  43.9 0.7 copy-start.4
  50.3 17.9 %collective-permute-start.2 = (bf16[2,4,80,512]{3,2,1,0:T(8,128)(2,1)S(1)}, bf16[2,4,80,512]{3,2,1,0:T(8,128)(2,1)S(1)}, u32[]{:S(2)}, u32[]{:S(2)}) collective-permute-start(bf16[2,4,80,512]{3,2,1,0:T(8,128)(2,1)S(1)} %pad_maximum_fusion), channel_id=1, source_target_pairs={{0,1},{1,2},{2,3},{4,5},{5,6},{6,7},{8,9},{9,10},{10,11},{12,13},{... | collective-permute-start | bytes 1966088 | tf_op jit(solution)/shard_map/ppermute | solution.py:297
  53.0 17.6 %collective-permute-start.3 = (bf16[2,4,80,512]{3,2,1,0:T(8,128)(2,1)S(1)}, bf16[2,4,80,512]{3,2,1,0:T(8,128)(2,1)S(1)}, u32[]{:S(2)}, u32[]{:S(2)}) collective-permute-start(bf16[2,4,80,512]{3,2,1,0:T(8,128)(2,1)S(1)} %pad_maximum_fusion.1), channel_id=1, source_target_pairs={{1,0},{2,1},{3,2},{5,4},{6,5},{7,6},{9,8},{10,9},{11,10},{13,12},{... | collective-permute-start | bytes 1966088 | tf_op jit(solution)/shard_map/ppermute | solution.py:297
  71.5 1.6 copy-start
  73.1 15.4 %collective-permute-start.5 = (bf16[4,2,2,80,128]{4,3,2,1,0:T(8,128)(2,1)S(1)}, bf16[4,2,2,80,128]{4,3,2,1,0:T(8,128)(2,1)S(1)}, u32[]{:S(2)}, u32[]{:S(2)}) collective-permute-start(bf16[4,2,2,80,128]{4,3,2,1,0:T(8,128)(2,1)S(1)} %slice_bitcast_fusion), channel_id=1, source_target_pairs={{16,0},{32,16},{48,32},{64,48},{80,64},{96,80},{112,96},{17,1},{33... | collective-permute-start | bytes 983048 | tf_op jit(solution)/shard_map/ppermute | solution.py:297
  88.5 0.8 copy-start.14
  99.6 2.6 %collective-permute-start.6 = (f32[1736,128]{1,0:T(8,128)}, f32[1736,128]{1,0:T(8,128)S(1)}, u32[]{:S(2)}, u32[]{:S(2)}) collective-permute-start(f32[1736,128]{1,0:T(8,128)} %get-tuple-element.20), channel_id=1, source_target_pairs={{0,128},{128,0},{1,129},{129,1},{2,130},{130,2},{3,131},{131,3},{4... | collective-permute-start | bytes 2666504 | tf_op jit(solution)/shard_map/ppermute | solution.py:292
  102.3 1.0 copy-start.6
  103.3 44.2 %copy-start.5 = (bf16[2,2,80,512]{3,2,0,1:T(8,128)(2,1)S(1)}, bf16[2,2,80,512]{3,2,0,1:T(8,128)(2,1)}, u32[]{:S(2)}) copy-start(bf16[2,2,80,512]{3,2,0,1:T(8,128)(2,1)} %copy-done.4) | copy-start | bytes 983044
  106.9 13.9 %collective-permute-start.7 = (bf16[288,128]{1,0:T(8,128)(2,1)S(1)}, bf16[288,128]{1,0:T(8,128)(2,1)S(1)}, u32[]{:S(2)}, u32[]{:S(2)}) collective-permute-start(bf16[288,128]{1,0:T(8,128)(2,1)S(1)} %get-tuple-element.39), channel_id=1, source_target_pairs={{0,16},{16,32},{32,48},{48,64},{64,80},{80,96},{96,112},{112,0},{1... | collective-permute-start | bytes 221192 | tf_op jit(solution)/shard_map/ppermute | solution.py:292
  108.9 14.3 %collective-permute-start.8 = (bf16[288,128]{1,0:T(8,128)(2,1)S(1)}, bf16[288,128]{1,0:T(8,128)(2,1)S(1)}, u32[]{:S(2)}, u32[]{:S(2)}) collective-permute-start(bf16[288,128]{1,0:T(8,128)(2,1)S(1)} %get-tuple-element.38), channel_id=1, source_target_pairs={{0,32},{16,48},{32,64},{48,80},{64,96},{80,112},{96,0},{112,16},{1... | collective-permute-start | bytes 221192 | tf_op jit(solution)/shard_map/ppermute | solution.py:292
  113.4 14.0 %collective-permute-start.9 = (bf16[288,128]{1,0:T(8,128)(2,1)S(1)}, bf16[288,128]{1,0:T(8,128)(2,1)S(1)}, u32[]{:S(2)}, u32[]{:S(2)}) collective-permute-start(bf16[288,128]{1,0:T(8,128)(2,1)S(1)} %get-tuple-element.37), channel_id=1, source_target_pairs={{0,48},{16,64},{32,80},{48,96},{64,112},{80,0},{96,16},{112,32},{1... | collective-permute-start | bytes 221192 | tf_op jit(solution)/shard_map/ppermute | solution.py:292
  116.3 11.1 %collective-permute-start.10 = (bf16[288,128]{1,0:T(8,128)(2,1)S(1)}, bf16[288,128]{1,0:T(8,128)(2,1)S(1)}, u32[]{:S(2)}, u32[]{:S(2)}) collective-permute-start(bf16[288,128]{1,0:T(8,128)(2,1)S(1)} %get-tuple-element.36), channel_id=1, source_target_pairs={{0,64},{16,80},{32,96},{48,112},{64,0},{80,16},{96,32},{112,48},{1... | collective-permute-start | bytes 221192 | tf_op jit(solution)/shard_map/ppermute | solution.py:292
  116.8 12.5 %collective-permute-start.11 = (bf16[288,128]{1,0:T(8,128)(2,1)S(1)}, bf16[288,128]{1,0:T(8,128)(2,1)S(1)}, u32[]{:S(2)}, u32[]{:S(2)}) collective-permute-start(bf16[288,128]{1,0:T(8,128)(2,1)S(1)} %get-tuple-element.35), channel_id=1, source_target_pairs={{0,80},{16,96},{32,112},{48,0},{64,16},{80,32},{96,48},{112,64},{1... | collective-permute-start | bytes 221192 | tf_op jit(solution)/shard_map/ppermute | solution.py:292
  120.8 13.0 %copy-start.7 = (bf16[288,128]{1,0:T(8,128)(2,1)}, bf16[288,128]{1,0:T(8,128)(2,1)S(1)}, u32[]{:S(2)}) copy-start(bf16[288,128]{1,0:T(8,128)(2,1)S(1)} %collective-permute-done.7.refs_0_) | copy-start | bytes 221188
  120.8 12.1 %collective-permute-start.12 = (bf16[288,128]{1,0:T(8,128)(2,1)S(1)}, bf16[288,128]{1,0:T(8,128)(2,1)S(1)}, u32[]{:S(2)}, u32[]{:S(2)}) collective-permute-start(bf16[288,128]{1,0:T(8,128)(2,1)S(1)} %get-tuple-element.34), channel_id=1, source_target_pairs={{0,96},{16,112},{32,0},{48,16},{64,32},{80,48},{96,64},{112,80},{1... | collective-permute-start | bytes 221192 | tf_op jit(solution)/shard_map/ppermute | solution.py:292
  123.2 10.6 %copy-start.8 = (bf16[288,128]{1,0:T(8,128)(2,1)}, bf16[288,128]{1,0:T(8,128)(2,1)S(1)}, u32[]{:S(2)}) copy-start(bf16[288,128]{1,0:T(8,128)(2,1)S(1)} %collective-permute-done.8.refs_1_) | copy-start | bytes 221188
  123.2 10.6 %collective-permute-start.13 = (bf16[288,128]{1,0:T(8,128)(2,1)S(1)}, bf16[288,128]{1,0:T(8,128)(2,1)S(1)}, u32[]{:S(2)}, u32[]{:S(2)}) collective-permute-start(bf16[288,128]{1,0:T(8,128)(2,1)S(1)} %get-tuple-element.33), channel_id=1, source_target_pairs={{0,112},{16,0},{32,16},{48,32},{64,48},{80,64},{96,80},{112,96},{1... | collective-permute-start | bytes 221192 | tf_op jit(solution)/shard_map/ppermute | solution.py:292
  127.4 6.4 %copy-start.9 = (bf16[288,128]{1,0:T(8,128)(2,1)}, bf16[288,128]{1,0:T(8,128)(2,1)S(1)}, u32[]{:S(2)}) copy-start(bf16[288,128]{1,0:T(8,128)(2,1)S(1)} %collective-permute-done.9.refs_2_) | copy-start | bytes 221188
  127.4 6.4 %copy-start.10 = (bf16[288,128]{1,0:T(8,128)(2,1)}, bf16[288,128]{1,0:T(8,128)(2,1)S(1)}, u32[]{:S(2)}) copy-start(bf16[288,128]{1,0:T(8,128)(2,1)S(1)} %collective-permute-done.10.refs_3_) | copy-start | bytes 221188
  129.3 4.5 %copy-start.11 = (bf16[288,128]{1,0:T(8,128)(2,1)}, bf16[288,128]{1,0:T(8,128)(2,1)S(1)}, u32[]{:S(2)}) copy-start(bf16[288,128]{1,0:T(8,128)(2,1)S(1)} %collective-permute-done.11.refs_4_) | copy-start | bytes 221188
  133.0 0.8 copy-start.12
  133.8 0.6 copy-start.13
  136.6 24.0 %all-to-all-start.1 = ((f32[16,72,128]{2,1,0:T(8,128)}), f32[16,72,128]{2,1,0:T(8,128)S(1)}, u32[]{:S(2)}, u32[]{:S(2)}) async-start(f32[16,72,128]{2,1,0:T(8,128)} %sum.1), calls=%async_computation.1 | async-start | bytes 1179648 | tf_op jit(solution)/shard_map/all_to_all | solution.py:404
  160.6 0.8 copy-start.1

commit v2 on v1

--- a/solution.py
+++ b/solution.py
@@ -28,7 +28,17 @@
     return scale, floats * scale
 
 
-def act_kernel(lat_ref, gain_ref, grad_ref, act_ref, mix_ref):
+def spread_kernel(grad_ref, mix_ref):
+    for j in range(4):
+        rows = pl.ds(COLS * j, COLS)
+        grad = grad_ref[rows, :].astype(F32)
+        for k in range(4):
+            piece = class_of(grad, k).astype(BF16)
+            for other in range(4):
+                mix_ref[4 * k + other, rows, :] = piece
+
+
+def act_kernel(lat_ref, gain_ref, act_ref, mix_ref):
     for j in range(4):
         rows = pl.ds(COLS * j, COLS)
         floats = lat_ref[rows, :].astype(F32)
@@ -36,13 +46,10 @@
         pre_act = normed * gain_ref[...]
         act = pre_act / (1.0 + jnp.exp(-pre_act))
         act_ref[rows, :] = act.astype(BF16)
-        grad = grad_ref[rows, :].astype(F32)
         for k in range(4):
-            act_piece = class_of(act, k).astype(BF16)
-            grad_piece = class_of(grad, k).astype(BF16)
+            piece = class_of(act, k).astype(BF16)
             for other in range(4):
-                mix_ref[4 * other + k, 0, rows, :] = act_piece
-                mix_ref[4 * k + other, 1, rows, :] = grad_piece
+                mix_ref[4 * other + k, rows, :] = piece
 
 
 def shifted_columns(block):
@@ -167,7 +174,7 @@
             sums_ref[pl.ds(4 + part, 1), :] = bias_sum[:, 128 * part : 128 * part + 128]
 
 
-def weight_kernel(mix_ref, halo_ref, sums_ref, keep_ref, send_ref, acts, grads, acc):
+def weight_kernel(act_ref, grad_ref, halo_ref, sums_ref, keep_ref, send_ref, acts, grads, acc):
     grad_scale = 1.0 / (TOTAL**0.5)
     zero = jnp.zeros((10, COLS, 128), BF16)
     grads[:, pl.ds(0, 1)] = zero.reshape(10, 1, COLS, 128)
@@ -177,8 +184,8 @@
             for f in range(2):
                 for r in range(2):
                     row = 2 * x + r
-                    grads[2 * y + f, 1 + row] = mix_ref[4 * y + x, 1, f, r]
-                    block = mix_ref[4 * y + x, 0, f, r]
+                    grads[2 * y + f, 1 + row] = grad_ref[4 * y + x, f, r]
+                    block = act_ref[4 * y + x, f, r]
                     for c, shifted in enumerate(shifted_columns(block)):
                         acts[y, c, pl.ds(640 * f + COLS * row, COLS), :] = shifted
     for x in range(4):
@@ -216,71 +223,59 @@
     send_ref[pl.ds(1728, 8), :] = sums_ref[...] * grad_scale
 
 
-def first_tap(z, x):
-    return jnp.minimum(lax.div(lax.div(27 * z - x + 3, 4), 2), 23)
-
-
-def split_kernel(keep_ref, got_ref, piece_ref, mine_ref, both):
-    both[...] = keep_ref[...] + got_ref[...]
-    z, x = lax.axis_index("z"), lax.axis_index("x")
+def first_unit(index, x):
+    return lax.div(lax.div(27 * index, 4) - x + 3, 4)
+
+
+def split_kernel(keep_ref, got_ref, piece_ref, both):
+    both[pl.ds(0, 1736), :] = keep_ref[...] + got_ref[...]
+    x = lax.axis_index("x")
     total = both[pl.ds(1728, 8), :]
     high = total.astype(BF16).astype(F32)
-    mid = (total - high).astype(BF16).astype(F32)
-    low = total - high - mid
-    terms = jnp.concatenate([high, mid, low, jnp.zeros_like(low)], axis=0).astype(BF16)
-    for k in range(8):
-        target = lax.rem(z + k, 8)
-        start = pl.multiple_of(64 * first_tap(target, x), 64)
-        if k == 0:
-            mine_ref[pl.ds(0, 256), :] = both[pl.ds(start, 256), :]
-            mine_ref[pl.ds(256, 8), :] = total
-        else:
-            piece_ref[k - 1, pl.ds(0, 256), :] = both[pl.ds(start, 256), :].astype(BF16)
-            piece_ref[k - 1, pl.ds(256, 32), :] = terms
-
-
-def sum_kernel(mine_ref, *refs):
-    got_refs, out_ref, taps = refs[:7], refs[7], refs[8]
-    z, x = lax.axis_index("z"), lax.axis_index("x")
-    block = mine_ref[pl.ds(0, 256), :]
-    total = mine_ref[pl.ds(256, 8), :]
-    for got in got_refs:
-        block += got[pl.ds(0, 256), :].astype(F32)
-        terms = got[pl.ds(256, 32), :].astype(F32)
-        total += terms[0:8] + terms[8:16] + terms[16:24]
-    taps[...] = block
+    terms = jnp.concatenate([high, total - high], axis=0).astype(BF16)
     lane = lax.broadcasted_iota(jnp.int32, (64, 128), 1)
+    for index in range(32):
+        unit = first_unit(index, x)
+        row = pl.multiple_of(64 * lax.div(unit, 2), 64)
+        here = both[pl.ds(row, 64), :]
+        after = both[pl.ds(row + 64, 64), :]
+        crossed = pltpu.roll(jnp.where(lane >= 64, here, after), 64, 1)
+        piece = jnp.where(lax.rem(unit, 2) == 1, crossed, here)
+        piece_ref[index, pl.ds(0, 64), :] = piece.astype(BF16)
+        piece_ref[index, pl.ds(64, 16), :] = terms
+
+
+def sum_kernel(got_ref, out_ref):
+    total = jnp.zeros((8, 128), F32)
+    parts = []
     for y in range(4):
-        group = lax.div(27 * (4 * z + y), 4)
-        unit = lax.div(group - x + 3, 4)
-        tap = lax.div(unit, 2) - first_tap(z, x)
-        odd = lax.rem(unit, 2)
-        here = taps[pl.ds(pl.multiple_of(64 * jnp.minimum(tap, 3), 64), 64), :]
-        after = taps[pl.ds(pl.multiple_of(64 * jnp.minimum(tap + 1, 3), 64), 64), :]
-        crossed = pltpu.roll(jnp.where(lane >= 64, here, after), 64, 1)
-        piece = jnp.where(odd == 1, crossed, here)
-        for other in range(4):
-            out_ref[4 * y + other, pl.ds(0, 64), :] = piece
-            out_ref[4 * y + other, pl.ds(64, 8), :] = total
-
-
-def final_kernel(got_ref, out_ref, sums_ref, rows):
-    z, y = lax.axis_index("z"), lax.axis_index("y")
+        block = jnp.zeros((64, 128), F32)
+        for z in range(8):
+            block += got_ref[4 * z + y, pl.ds(0, 64), :].astype(F32)
+            terms = got_ref[4 * z + y, pl.ds(64, 16), :].astype(F32)
+            total += terms[0:8] + terms[8:16]
+        parts.append(block)
+    for unit in range(2):
+        lanes = slice(64 * unit, 64 * unit + 64)
+        out_ref[pl.ds(64 * unit, 64), :] = jnp.concatenate([p[:, lanes] for p in parts], axis=-1)
+    out_ref[pl.ds(128, 8), :] = jnp.concatenate([total, total], axis=-1)
+
+
+def final_kernel(own_ref, one_ref, two_ref, three_ref, out_ref, sums_ref, held, rows):
+    z, y, x = lax.axis_index("z"), lax.axis_index("y"), lax.axis_index("x")
     index = 4 * z + y
     group = lax.div(27 * index, 4)
+    total = jnp.zeros((8, 128), F32)
+    for k, ref in enumerate((own_ref, one_ref, two_ref, three_ref)):
+        held[lax.rem(x - k + 4, 4)] = ref[...]
+    for k in range(4):
+        total += held[k, pl.ds(128, 8), pl.ds(0, 128)]
+    sums_ref[...] = total
     for j in range(8):
         source = lax.rem(group + j, 4)
-        pieces = []
-        for part in range(4):
-            block = got_ref[4 * part + source, pl.ds(0, 64), :]
-            pieces.append(block[:, :64] if j < 4 else block[:, 64:])
-        rows[pl.ds(64 * j, 64), :] = jnp.concatenate(pieces, axis=-1)
+        rows[pl.ds(64 * j, 64), :] = held[source, pl.ds(64 * (j // 4), 64), :]
     offset = pl.multiple_of(16 * lax.rem(27 * index, 4), 16)
     out_ref[...] = rows[pl.ds(offset, 432), :]
-    total = got_ref[0, pl.ds(64, 8), :]
-    for k in range(1, 16):
-        total += got_ref[k, pl.ds(64, 8), :]
-    sums_ref[...] = total
 
 
 def shape(dims, dtype):
@@ -309,25 +304,29 @@
 
     kernel_other = moved(kernel, "dp", 1)
     later = neighbour(grad, ("z", "y"), 32, -1)
-
-    act_flat, mix = pl.pallas_call(
+    grad_mix = pl.pallas_call(
+        spread_kernel,
+        out_shape=shape((16, CELLS, 128), BF16),
+        compiler_params=BIG,
+        name="spread",
+    )(grad.reshape(CELLS, CH))
+    grad_mix = lax.all_to_all(grad_mix, ("y", "x"), 0, 0).reshape(16, 2, 2, COLS, 128)
+    act_flat, act_mix = pl.pallas_call(
         act_kernel,
-        out_shape=(shape((CELLS, CH), BF16), shape((16, 2, CELLS, 128), BF16)),
+        out_shape=(shape((CELLS, CH), BF16), shape((16, CELLS, 128), BF16)),
         compiler_params=BIG,
         name="act",
-    )(lat_flat, gain_row, grad.reshape(CELLS, CH))
+    )(lat_flat, gain_row)
     act = act_flat.reshape(2, 2, COLS, CH)
-    earlier = neighbour(act, ("z", "y"), 32, 1)
-
-    mixed = lax.all_to_all(mix, ("y", "x"), 0, 0).reshape(16, 2, 2, 2, COLS, 128)
-    halo = neighbour(mixed[0:4, 1], "z", 8, -1)
-
-    frames_grad = jnp.concatenate([grad, later], axis=0)
-    frames_act = jnp.concatenate([earlier, act], axis=0)
-    edge_up = jnp.stack([frames_grad[:, 1], frames_act[:, 1]])
-    edge_down = jnp.stack([frames_grad[:, 0], frames_act[:, 0]])
-    low = neighbour(edge_up, "x", 4, 1)
-    high = neighbour(edge_down, "x", 4, -1)
+    act_mix = lax.all_to_all(act_mix, ("y", "x"), 0, 0).reshape(16, 2, 2, COLS, 128)
+    halo = neighbour(grad_mix[0:4], "z", 8, -1)
+    grad_low = neighbour(jnp.concatenate([grad[:, 1], later[:, 1]]), "x", 4, 1)
+    grad_high = neighbour(jnp.concatenate([grad[:, 0], later[:, 0]]), "x", 4, -1)
+
+    act_late, act_mix = lax.optimization_barrier((act, act_mix))
+    earlier = neighbour(act_late, ("z", "y"), 32, 1)
+    act_low = neighbour(jnp.concatenate([earlier[:, 1], act_late[:, 1]]), "x", 4, 1)
+    act_high = neighbour(jnp.concatenate([earlier[:, 0], act_late[:, 0]]), "x", 4, -1)
 
     weight_specs = [pl.BlockSpec((3 * CH, HALF), lambda i: (i, 0))] * 2
     tile = (2, 2, COLS, CH)
@@ -349,7 +348,7 @@
             flops=2 * CELLS * 27 * CH * CH, bytes_accessed=16_000_000, transcendentals=0
         ),
         name="back",
-    )(lat_flat, gain_row, grad, later, low[0], high[0], kernel, kernel_other)
+    )(lat_flat, gain_row, grad, later, grad_low, grad_high, kernel, kernel_other)
 
     block_out = pl.pallas_call(
         conv_kernel,
@@ -368,7 +367,7 @@
             flops=2 * CELLS * 27 * CH * CH, bytes_accessed=16_000_000, transcendentals=0
         ),
         name="conv",
-    )(lat_flat, bias_row, act, earlier, low[1], high[1], kernel, kernel_other)
+    )(lat_flat, bias_row, act, earlier, act_low, act_high, kernel, kernel_other)
 
     keep, send = pl.pallas_call(
         weight_kernel,
@@ -383,32 +382,31 @@
             flops=2 * CELLS * 27 * CH * CH, bytes_accessed=5_000_000, transcendentals=0
         ),
         name="weight",
-    )(mixed, halo, sums)
+    )(act_mix, grad_mix, halo, sums)
     got = moved(send, "dp", 1)
 
-    pieces, mine = pl.pallas_call(
+    pieces = pl.pallas_call(
         split_kernel,
-        out_shape=(shape((7, 288, 128), BF16), shape((264, 128), F32)),
-        scratch_shapes=[pltpu.VMEM((1736, 128), F32)],
+        out_shape=shape((32, 80, 128), BF16),
+        scratch_shapes=[pltpu.VMEM((1792, 128), F32)],
         compiler_params=BIG,
         name="split",
     )(keep, got)
-    arrived = [moved(pieces[k - 1], "z", k) for k in range(1, 8)]
-    spread = pl.pallas_call(
+    pieces = lax.all_to_all(pieces, ("z", "y"), 0, 0)
+    summed = pl.pallas_call(
         sum_kernel,
-        out_shape=shape((16, 72, 128), F32),
-        scratch_shapes=[pltpu.VMEM((256, 128), F32)],
+        out_shape=shape((136, 256), F32),
         compiler_params=BIG,
         name="sum",
-    )(mine, *arrived)
-    gathered = lax.all_to_all(spread, ("y", "x"), 0, 0)
+    )(pieces)
+    around = [moved(summed, "x", k) for k in range(1, 4)]
     kernel_grad, totals = pl.pallas_call(
         final_kernel,
         out_shape=(shape((432, 256), F32), shape((8, 128), F32)),
-        scratch_shapes=[pltpu.VMEM((512, 256), F32)],
+        scratch_shapes=[pltpu.VMEM((4, 136, 256), F32), pltpu.VMEM((512, 256), F32)],
         compiler_params=BIG,
         name="final",
-    )(gathered)
+    )(summed, *around)
     return (
         block_out.reshape(latents.shape),
         latent_grad.reshape(latents.shape),

time: 166 us -> 176 us (1.060)
  waiting for transfers between devices: 53.3 us -> 67.3 us
  starting transfers between devices: 52.9 us -> 49.2 us
  local copies, waits for them, and re-layouts: 11.4 us -> 8.4 us
    all_to_all x2 -> x3, waiting for transfers between devices: 0.01 us -> 17.1 us  [the longest x1 17.1 us: on_device(): lax.all_to_all(act_mix, ('y', 'x'), 0, 0).reshape(16, 2, 2, COLS, 128)]
    ppermute x9 -> x5, starting transfers between devices: 18.6 us -> 2.86 us  [moved(): lax.ppermute(block, axis, [(i, (i + distance) % count) for i in range(cou...]
    ppermute x9 -> x5, waiting for transfers between devices: 11 us -> 2.65 us  [moved(): lax.ppermute(block, axis, [(i, (i + distance) % count) for i in range(cou...]
    all_to_all x2 -> x3, starting transfers between devices: 18.5 us -> 25 us  [the longest x1 10.9 us: on_device(): pieces = lax.all_to_all(pieces, ('z', 'y'), 0, 0)]
    ppermute x5 -> x7, starting transfers between devices: 15.8 us -> 21.3 us  [neighbour(): return lax.ppermute(block, axes, route)]
    ppermute x5 -> x7, waiting for transfers between devices: 42.3 us -> 47.5 us  [neighbour(): return lax.ppermute(block, axes, route)]
    squeeze x4, local copies, waits for them, and re-layouts: 2.96 us -> 0.09 us  [the longest x1 0.02 us: on_device(): grad[:, 0]]
    pallas_call x2 -> x3, Pallas kernels: 4.68 us -> 6.79 us  [the longest x1 2.68 us: on_device(): pl.pallas_call(split_kernel, out_shape=shape((32, 80, 128), BF16), scratc...]
  transfers between devices with their start and end apart: 16 -> 15, of which waited for: 9 -> 7; matrix products, arithmetic and copies ran while one was open for 2% -> 1% of each run, Pallas kernels for 18% -> 19%
where the time goes in v2:
time: 176 us; the launch traced here: 173 us
  waiting for transfers between devices  67.3 us (38%)
  starting transfers between devices  49.2 us (28%)
  Pallas kernels  47.4 us (27%)
  local copies, waits for them, and re-layouts  8.4 us (5%)
    ppermute x7, waiting for transfers between devices, neighbour(): return lax.ppermute(block, axes, route)  47.5 us
    ppermute x7, starting transfers between devices, neighbour(): return lax.ppermute(block, axes, route)  21.3 us
    all_to_all x1, waiting for transfers between devices, on_device(): lax.all_to_all(act_mix, ('y', 'x'), 0, 0).reshape(16, 2, 2, COLS, 128)  17.1 us
    pallas_call x1, Pallas kernels, on_device(): pl.pallas_call(back_kernel, grid=(9,), in_specs=[whole((CELLS, CH)), whol...  13.4 us
    pallas_call x1, Pallas kernels, on_device(): pl.pallas_call(conv_kernel, grid=(9,), in_specs=[whole((CELLS, CH)), whol...  12.4 us
    all_to_all x1, starting transfers between devices, on_device(): pieces = lax.all_to_all(pieces, ('z', 'y'), 0, 0)  10.9 us
    pallas_call x1, Pallas kernels, on_device(): pl.pallas_call(weight_kernel, out_shape=(shape((1736, 128), F32), shape((...  10.3 us
    all_to_all x1, starting transfers between devices, on_device(): lax.all_to_all(act_mix, ('y', 'x'), 0, 0).reshape(16, 2, 2, COLS, 128)  7.48 us
  transfers between devices with their start and end apart: 15, of which 7 were waited for; matrix products, arithmetic and copies ran while one was open for 1% of the time, Pallas kernels for 19%

profile of v2, /device:TPU:34, one launch (start us, length us, event | category | flops | bytes accessed | tf_op | source)
XLA Modules:
  0.0 173.3 jit_solution(8822772418765762765)
XLA Ops:
  0.6 0.1 collective-permute-start.3
  0.7 2.7 %act.1 = (bf16[320,512]{1,0:T(8,128)(2,1)}, bf16[16,320,128]{2,1,0:T(8,128)(2,1)}) custom-call(bf16[320,512]{1,0:T(8,128)(2,1)} %bitcast.43, f32[1,512]{1,0:T(1,128)} %bitcast.47), custom_call_target="tpu_custom_call" | custom-call | tf_op jit(solution)/shard_map/act/pallas_call | solution.py:314
  3.4 7.5 %all-to-all-start = ((bf16[16,320,128]{2,1,0:T(8,128)(2,1)}), bf16[16,320,128]{2,1,0:T(8,128)(2,1)S(1)}, u32[]{:S(2)}, u32[]{:S(2)}) async-start(bf16[16,320,128]{2,1,0:T(8,128)(2,1)} %get-tuple-element.16), calls=%async_computation | async-start | bytes 2621440 | tf_op jit(solution)/shard_map/all_to_all | solution.py:321
  10.9 2.2 %spread.1 = bf16[16,320,128]{2,1,0:T(8,128)(2,1)} custom-call(bf16[320,512]{1,0:T(8,128)(2,1)} %bitcast.41), custom_call_target="tpu_custom_call" | custom-call | tf_op jit(solution)/shard_map/spread/pallas_call | solution.py:307
  13.1 17.1 %all-to-all-done = bf16[16,320,128]{2,1,0:T(8,128)(2,1)S(1)} async-done(((bf16[16,320,128]{2,1,0:T(8,128)(2,1)}), bf16[16,320,128]{2,1,0:T(8,128)(2,1)S(1)}, u32[]{:S(2)}, u32[]{:S(2)}) %all-to-all-start) | async-done | bytes 1310752 | tf_op jit(solution)/shard_map/all_to_all | solution.py:321
  30.2 0.0 copy-start.2
  30.2 6.6 %all-to-all-start.1 = ((bf16[16,320,128]{2,1,0:T(8,128)(2,1)}), bf16[16,320,128]{2,1,0:T(8,128)(2,1)S(1)}, u32[]{:S(2)}, u32[]{:S(2)}) async-start(bf16[16,320,128]{2,1,0:T(8,128)(2,1)} %spread.1), calls=%async_computation.1 | async-start | bytes 2621440 | tf_op jit(solution)/shard_map/all_to_all | solution.py:313
  36.8 0.0 copy-done.4
  36.9 0.0 copy-done.2
  36.9 4.2 %collective-permute-start.4 = (bf16[2,2,80,512]{3,2,0,1:T(8,128)(2,1)S(1)}, bf16[2,2,80,512]{3,2,0,1:T(8,128)(2,1)S(1)}, u32[]{:S(2)}, u32[]{:S(2)}) collective-permute-start(bf16[2,2,80,512]{3,2,0,1:T(8,128)(2,1)S(1)} %bitcast.39), channel_id=1, source_target_pairs={{4,0},{8,4},{12,8},{16,12},{20,16},{24,20},{28,24},{32,28},{36,32}... | collective-permute-start | bytes 983048 | tf_op jit(solution)/shard_map/ppermute | solution.py:292
  41.1 18.4 %collective-permute-done.4 = bf16[2,2,80,512]{3,2,0,1:T(8,128)(2,1)S(1)} collective-permute-done((bf16[2,2,80,512]{3,2,0,1:T(8,128)(2,1)S(1)}, bf16[2,2,80,512]{3,2,0,1:T(8,128)(2,1)S(1)}, u32[]{:S(2)}, u32[]{:S(2)}) %collective-permute-start.4) | collective-permute-done | bytes 327712 | tf_op jit(solution)/shard_map/ppermute | solution.py:292
  59.6 3.4 %collective-permute-start.5 = (bf16[4,80,512]{2,1,0:T(8,128)(2,1)S(1)}, bf16[4,80,512]{2,1,0:T(8,128)(2,1)S(1)}, u32[]{:S(2)}, u32[]{:S(2)}) collective-permute-start(bf16[4,80,512]{2,1,0:T(8,128)(2,1)S(1)} %pad_maximum_fusion.2), channel_id=1, source_target_pairs={{0,1},{1,2},{2,3},{4,5},{5,6},{6,7},{8,9},{9,10},{10,11},{12,13},{... | collective-permute-start | bytes 983048 | tf_op jit(solution)/shard_map/ppermute | solution.py:292
  63.0 2.5 %collective-permute-start.6 = (bf16[4,80,512]{2,1,0:T(8,128)(2,1)S(1)}, bf16[4,80,512]{2,1,0:T(8,128)(2,1)S(1)}, u32[]{:S(2)}, u32[]{:S(2)}) collective-permute-start(bf16[4,80,512]{2,1,0:T(8,128)(2,1)S(1)} %pad_maximum_fusion.3), channel_id=1, source_target_pairs={{1,0},{2,1},{3,2},{5,4},{6,5},{7,6},{9,8},{10,9},{11,10},{13,12},{... | collective-permute-start | bytes 983048 | tf_op jit(solution)/shard_map/ppermute | solution.py:292
  65.5 0.7 copy.21.next_ref
  66.3 0.0 all-to-all-done.1
  66.3 0.0 copy-start.1
  66.3 2.0 %collective-permute-start.7 = (bf16[4,2,2,80,128]{4,3,2,1,0:T(8,128)(2,1)S(1)}, bf16[4,2,2,80,128]{4,3,2,1,0:T(8,128)(2,1)S(1)}, u32[]{:S(2)}, u32[]{:S(2)}) collective-permute-start(bf16[4,2,2,80,128]{4,3,2,1,0:T(8,128)(2,1)S(1)} %bitcast.46), channel_id=1, source_target_pairs={{16,0},{32,16},{48,32},{64,48},{80,64},{96,80},{112,96},{17,1},{33... | collective-permute-start | bytes 983048 | tf_op jit(solution)/shard_map/ppermute | solution.py:292
  68.3 1.3 collective-permute-done.5.low_ref
  69.6 3.7 %collective-permute-done.6.high_ref = bf16[4,80,512]{2,1,0:T(8,128)(2,1)S(1)} collective-permute-done((bf16[4,80,512]{2,1,0:T(8,128)(2,1)S(1)}, bf16[4,80,512]{2,1,0:T(8,128)(2,1)S(1)}, u32[]{:S(2)}, u32[]{:S(2)}) %collective-permute-start.6) | collective-permute-done | bytes 327712 | tf_op jit(solution)/shard_map/ppermute | solution.py:292
  73.3 0.0 copy-start.12
  73.3 0.0 collective-permute-done.3.oth_ref
  73.3 0.0 copy-done.10
  73.3 0.7 copy-done.12
  74.1 13.4 %back.1 = (bf16[320,512]{1,0:T(8,128)(2,1)}, f32[8,128]{1,0:T(8,128)}) custom-call(bf16[320,512]{1,0:T(8,128)(2,1)} %bitcast.44, f32[1,512]{1,0:T(1,128)} %bitcast.48, bf16[2,2,80,512]{3,2,1,0:T(8,128)(2,1)} %bitcast.42, bf16[2,2,80,512]{3,2,1,0:T(8,128)(2,1)} %copy.21.next_ref, bf16[4,80,512]{2,1,0:T(8,128)(2,1)} %copy-done.10, ...), custom_call_target="tpu_custom_call" | custom-call | flops 4529848320 | bytes 16000000 | tf_op jit(solution)/shard_map/back/pallas_call | solution.py:334
  87.4 0.0 copy-done.1
  87.4 0.0 collective-permute-done.7.halo_ref
  87.4 0.0 copy-start.13
  87.5 0.7 copy-done.13
  88.2 10.3 %weight.1 = (f32[1736,128]{1,0:T(8,128)}, f32[1736,128]{1,0:T(8,128)}) custom-call(bf16[16,2,2,80,128]{4,3,2,1,0:T(8,128)(2,1)} %bitcast.35, bf16[16,2,2,80,128]{4,3,2,1,0:T(8,128)(2,1)} %bitcast.34, bf16[4,2,2,80,128]{4,3,2,1,0:T(8,128)(2,1)} %copy-done.13, f32[8,128]{1,0:T(8,128)} %get-tuple-element.20.sums_ref), custom_call_target="tpu_custom_call" | custom-call | flops 4529848320 | bytes 5000000 | tf_op jit(solution)/shard_map/weight/pallas_call | solution.py:372
  98.5 0.0 collective-permute-start.8
  98.5 2.6 %collective-permute-done.8.got_ref = f32[1736,128]{1,0:T(8,128)S(1)} collective-permute-done((f32[1736,128]{1,0:T(8,128)}, f32[1736,128]{1,0:T(8,128)S(1)}, u32[]{:S(2)}, u32[]{:S(2)}) %collective-permute-start.8) | collective-permute-done | bytes 888864 | tf_op jit(solution)/shard_map/ppermute | solution.py:287
  101.1 0.0 copy-start.5
  101.1 1.0 copy-done.5
  102.1 0.0 copy-start.3
  102.1 2.7 %split.1 = bf16[32,80,128]{2,1,0:T(8,128)(2,1)} custom-call(f32[1736,128]{1,0:T(8,128)} %get-tuple-element.21.keep_ref, f32[1736,128]{1,0:T(8,128)} %copy-done.5), custom_call_target="tpu_custom_call" | custom-call | tf_op jit(solution)/shard_map/split/pallas_call | solution.py:388
  104.7 10.9 %all-to-all-start.2 = ((bf16[32,80,128]{2,1,0:T(8,128)(2,1)}), bf16[32,80,128]{2,1,0:T(8,128)(2,1)S(1)}, u32[]{:S(2)}, u32[]{:S(2)}) async-start(bf16[32,80,128]{2,1,0:T(8,128)(2,1)} %split.1), calls=%async_computation.2 | async-start | bytes 1310720 | tf_op jit(solution)/shard_map/all_to_all | solution.py:395
  115.6 0.0 copy-done.3
  115.7 3.4 %collective-permute-start = (bf16[2,2,80,512]{3,2,0,1:T(8,128)(2,1)S(1)}, bf16[2,2,80,512]{3,2,0,1:T(8,128)(2,1)S(1)}, u32[]{:S(2)}, u32[]{:S(2)}) collective-permute-start(bf16[2,2,80,512]{3,2,0,1:T(8,128)(2,1)S(1)} %copy.15), channel_id=1, source_target_pairs={{0,4},{4,8},{8,12},{12,16},{16,20},{20,24},{24,28},{28,32},{32,36}... | collective-permute-start | bytes 983048 | tf_op jit(solution)/shard_map/ppermute | solution.py:292
  119.1 21.0 %collective-permute-done = bf16[2,2,80,512]{3,2,0,1:T(8,128)(2,1)S(1)} collective-permute-done((bf16[2,2,80,512]{3,2,0,1:T(8,128)(2,1)S(1)}, bf16[2,2,80,512]{3,2,0,1:T(8,128)(2,1)S(1)}, u32[]{:S(2)}, u32[]{:S(2)}) %collective-permute-start) | collective-permute-done | bytes 327712 | tf_op jit(solution)/shard_map/ppermute | solution.py:292
  140.2 2.6 %collective-permute-start.1 = (bf16[4,80,512]{2,1,0:T(8,128)(2,1)S(1)}, bf16[4,80,512]{2,1,0:T(8,128)(2,1)S(1)}, u32[]{:S(2)}, u32[]{:S(2)}) collective-permute-start(bf16[4,80,512]{2,1,0:T(8,128)(2,1)S(1)} %pad_maximum_fusion), channel_id=1, source_target_pairs={{0,1},{1,2},{2,3},{4,5},{5,6},{6,7},{8,9},{9,10},{10,11},{12,13},{... | collective-permute-start | bytes 983048 | tf_op jit(solution)/shard_map/ppermute | solution.py:292
  142.8 3.3 %collective-permute-start.2 = (bf16[4,80,512]{2,1,0:T(8,128)(2,1)S(1)}, bf16[4,80,512]{2,1,0:T(8,128)(2,1)S(1)}, u32[]{:S(2)}, u32[]{:S(2)}) collective-permute-start(bf16[4,80,512]{2,1,0:T(8,128)(2,1)S(1)} %pad_maximum_fusion.1), channel_id=1, source_target_pairs={{1,0},{2,1},{3,2},{5,4},{6,5},{7,6},{9,8},{10,9},{11,10},{13,12},{... | collective-permute-start | bytes 983048 | tf_op jit(solution)/shard_map/ppermute | solution.py:292
  146.1 0.8 copy.18.prev_ref
  146.9 0.0 all-to-all-done.2.got_ref
  146.9 0.0 copy-start
  146.9 0.9 copy-done
  147.7 1.9 %sum.1.own_ref = f32[136,256]{1,0:T(8,128)} custom-call(bf16[32,80,128]{2,1,0:T(8,128)(2,1)} %copy-done), custom_call_target="tpu_custom_call" | custom-call | tf_op jit(solution)/shard_map/sum/pallas_call | solution.py:396
  149.6 0.7 collective-permute-start.9
  150.3 0.8 collective-permute-start.10
  151.1 1.3 collective-permute-start.11
  152.4 0.0 collective-permute-done.1.low_ref
  152.4 0.0 copy-start.9
  152.4 3.1 %collective-permute-done.2.high_ref = bf16[4,80,512]{2,1,0:T(8,128)(2,1)S(1)} collective-permute-done((bf16[4,80,512]{2,1,0:T(8,128)(2,1)S(1)}, bf16[4,80,512]{2,1,0:T(8,128)(2,1)S(1)}, u32[]{:S(2)}, u32[]{:S(2)}) %collective-permute-start.2) | collective-permute-done | bytes 327712 | tf_op jit(solution)/shard_map/ppermute | solution.py:292
  155.5 0.0 copy-done.9
  155.5 0.8 copy-done.11
  156.2 12.4 %conv.1 = bf16[320,512]{1,0:T(8,128)(2,1)} custom-call(bf16[320,512]{1,0:T(8,128)(2,1)} %bitcast.45, f32[1,512]{1,0:T(1,128)} %bitcast.49, bf16[2,2,80,512]{3,2,1,0:T(8,128)(2,1)} %bitcast.36, bf16[2,2,80,512]{3,2,1,0:T(8,128)(2,1)} %copy.18.prev_ref, bf16[4,80,512]{2,1,0:T(8,128)(2,1)} %copy-done.9, bf16[4,80,512]{2,1,0:T(8,128)(2,1)} %copy-done.11, ...), custom_call_target="tpu_custom_call" | custom-call | flops 4529848320 | bytes 16000000 | tf_op jit(solution)/shard_map/conv/pallas_call | solution.py:353
  168.6 0.0 collective-permute-done.9.one_ref
  168.6 0.0 collective-permute-done.10.two_ref
  168.6 0.0 copy-start.7
  168.6 0.0 collective-permute-done.11.three_ref
  168.6 0.6 copy-done.6
  169.2 0.1 copy-done.7
  169.3 0.7 copy-done.8
  169.9 2.0 %final.1 = (f32[432,256]{1,0:T(8,128)}, f32[8,128]{1,0:T(8,128)}) custom-call(f32[136,256]{1,0:T(8,128)} %sum.1.own_ref, f32[136,256]{1,0:T(8,128)} %copy-done.6, f32[136,256]{1,0:T(8,128)} %copy-done.7, f32[136,256]{1,0:T(8,128)} %copy-done.8), custom_call_target="tpu_custom_call" | custom-call | tf_op jit(solution)/shard_map/final/pallas_call | solution.py:403
  171.9 1.3 slice_bitcast_fusion.8
  (16 shorter events, 0.3 us)
Async XLA Ops:
  0.6 72.7 %collective-permute-start.3 = (bf16[13824,256]{1,0:T(8,128)(2,1)}, bf16[13824,256]{1,0:T(8,128)(2,1)}, u32[]{:S(2)}, u32[]{:S(2)}) collective-permute-start(bf16[13824,256]{1,0:T(8,128)(2,1)} %own_ref.3), channel_id=1, source_target_pairs={{0,128},{128,0},{1,129},{129,1},{2,130},{130,2},{3,131},{131,3},{4... | collective-permute-start | bytes 21233672 | tf_op jit(solution)/shard_map/ppermute | solution.py:287
  3.4 26.8 %all-to-all-start = ((bf16[16,320,128]{2,1,0:T(8,128)(2,1)}), bf16[16,320,128]{2,1,0:T(8,128)(2,1)S(1)}, u32[]{:S(2)}, u32[]{:S(2)}) async-start(bf16[16,320,128]{2,1,0:T(8,128)(2,1)} %get-tuple-element.16), calls=%async_computation | async-start | bytes 2621440 | tf_op jit(solution)/shard_map/all_to_all | solution.py:321
  13.1 23.7 %copy-start.4 = (bf16[1,2,2,80,512]{4,3,2,1,0:T(8,128)(2,1)S(1)}, bf16[1,2,2,80,512]{4,3,2,1,0:T(8,128)(2,1)}, u32[]{:S(2)}) copy-start(bf16[1,2,2,80,512]{4,3,2,1,0:T(8,128)(2,1)} %param.9) | copy-start | bytes 983044
  30.2 6.7 %copy-start.2 = (bf16[16,320,128]{2,1,0:T(8,128)(2,1)}, bf16[16,320,128]{2,1,0:T(8,128)(2,1)S(1)}, u32[]{:S(2)}) copy-start(bf16[16,320,128]{2,1,0:T(8,128)(2,1)S(1)} %all-to-all-done) | copy-start | bytes 3932164
  30.2 36.0 %all-to-all-start.1 = ((bf16[16,320,128]{2,1,0:T(8,128)(2,1)}), bf16[16,320,128]{2,1,0:T(8,128)(2,1)S(1)}, u32[]{:S(2)}, u32[]{:S(2)}) async-start(bf16[16,320,128]{2,1,0:T(8,128)(2,1)} %spread.1), calls=%async_computation.1 | async-start | bytes 2621440 | tf_op jit(solution)/shard_map/all_to_all | solution.py:313
  36.9 22.6 %collective-permute-start.4 = (bf16[2,2,80,512]{3,2,0,1:T(8,128)(2,1)S(1)}, bf16[2,2,80,512]{3,2,0,1:T(8,128)(2,1)S(1)}, u32[]{:S(2)}, u32[]{:S(2)}) collective-permute-start(bf16[2,2,80,512]{3,2,0,1:T(8,128)(2,1)S(1)} %bitcast.39), channel_id=1, source_target_pairs={{4,0},{8,4},{12,8},{16,12},{20,16},{24,20},{28,24},{32,28},{36,32}... | collective-permute-start | bytes 983048 | tf_op jit(solution)/shard_map/ppermute | solution.py:292
  59.6 10.0 %collective-permute-start.5 = (bf16[4,80,512]{2,1,0:T(8,128)(2,1)S(1)}, bf16[4,80,512]{2,1,0:T(8,128)(2,1)S(1)}, u32[]{:S(2)}, u32[]{:S(2)}) collective-permute-start(bf16[4,80,512]{2,1,0:T(8,128)(2,1)S(1)} %pad_maximum_fusion.2), channel_id=1, source_target_pairs={{0,1},{1,2},{2,3},{4,5},{5,6},{6,7},{8,9},{9,10},{10,11},{12,13},{... | collective-permute-start | bytes 983048 | tf_op jit(solution)/shard_map/ppermute | solution.py:292
  63.0 10.3 %collective-permute-start.6 = (bf16[4,80,512]{2,1,0:T(8,128)(2,1)S(1)}, bf16[4,80,512]{2,1,0:T(8,128)(2,1)S(1)}, u32[]{:S(2)}, u32[]{:S(2)}) collective-permute-start(bf16[4,80,512]{2,1,0:T(8,128)(2,1)S(1)} %pad_maximum_fusion.3), channel_id=1, source_target_pairs={{1,0},{2,1},{3,2},{5,4},{6,5},{7,6},{9,8},{10,9},{11,10},{13,12},{... | collective-permute-start | bytes 983048 | tf_op jit(solution)/shard_map/ppermute | solution.py:292
  66.3 21.2 %copy-start.1 = (bf16[16,320,128]{2,1,0:T(8,128)(2,1)}, bf16[16,320,128]{2,1,0:T(8,128)(2,1)S(1)}, u32[]{:S(2)}) copy-start(bf16[16,320,128]{2,1,0:T(8,128)(2,1)S(1)} %all-to-all-done.1) | copy-start | bytes 3932164
  66.3 21.1 %collective-permute-start.7 = (bf16[4,2,2,80,128]{4,3,2,1,0:T(8,128)(2,1)S(1)}, bf16[4,2,2,80,128]{4,3,2,1,0:T(8,128)(2,1)S(1)}, u32[]{:S(2)}, u32[]{:S(2)}) collective-permute-start(bf16[4,2,2,80,128]{4,3,2,1,0:T(8,128)(2,1)S(1)} %bitcast.46), channel_id=1, source_target_pairs={{16,0},{32,16},{48,32},{64,48},{80,64},{96,80},{112,96},{17,1},{33... | collective-permute-start | bytes 983048 | tf_op jit(solution)/shard_map/ppermute | solution.py:292
  69.6 3.7 %copy-start.10 = (bf16[4,80,512]{2,1,0:T(8,128)(2,1)}, bf16[4,80,512]{2,1,0:T(8,128)(2,1)S(1)}, u32[]{:S(2)}) copy-start(bf16[4,80,512]{2,1,0:T(8,128)(2,1)S(1)} %collective-permute-done.5.low_ref) | copy-start | bytes 983044
  73.3 0.8 copy-start.12
  87.4 0.7 copy-start.13
  98.5 2.6 %collective-permute-start.8 = (f32[1736,128]{1,0:T(8,128)}, f32[1736,128]{1,0:T(8,128)S(1)}, u32[]{:S(2)}, u32[]{:S(2)}) collective-permute-start(f32[1736,128]{1,0:T(8,128)} %get-tuple-element.22), channel_id=1, source_target_pairs={{0,128},{128,0},{1,129},{129,1},{2,130},{130,2},{3,131},{131,3},{4... | collective-permute-start | bytes 2666504 | tf_op jit(solution)/shard_map/ppermute | solution.py:287
  101.1 1.0 copy-start.5
  102.1 13.6 %copy-start.3 = (bf16[320,512]{1,0:T(8,128)(2,1)S(1)}, bf16[320,512]{1,0:T(8,128)(2,1)}, u32[]{:S(2)}) copy-start(bf16[320,512]{1,0:T(8,128)(2,1)} %get-tuple-element.15) | copy-start | bytes 983044
  104.7 42.1 %all-to-all-start.2 = ((bf16[32,80,128]{2,1,0:T(8,128)(2,1)}), bf16[32,80,128]{2,1,0:T(8,128)(2,1)S(1)}, u32[]{:S(2)}, u32[]{:S(2)}) async-start(bf16[32,80,128]{2,1,0:T(8,128)(2,1)} %split.1), calls=%async_computation.2 | async-start | bytes 1310720 | tf_op jit(solution)/shard_map/all_to_all | solution.py:395
  115.7 24.4 %collective-permute-start = (bf16[2,2,80,512]{3,2,0,1:T(8,128)(2,1)S(1)}, bf16[2,2,80,512]{3,2,0,1:T(8,128)(2,1)S(1)}, u32[]{:S(2)}, u32[]{:S(2)}) collective-permute-start(bf16[2,2,80,512]{3,2,0,1:T(8,128)(2,1)S(1)} %copy.15), channel_id=1, source_target_pairs={{0,4},{4,8},{8,12},{12,16},{16,20},{20,24},{24,28},{28,32},{32,36}... | collective-permute-start | bytes 983048 | tf_op jit(solution)/shard_map/ppermute | solution.py:292
  140.2 12.2 %collective-permute-start.1 = (bf16[4,80,512]{2,1,0:T(8,128)(2,1)S(1)}, bf16[4,80,512]{2,1,0:T(8,128)(2,1)S(1)}, u32[]{:S(2)}, u32[]{:S(2)}) collective-permute-start(bf16[4,80,512]{2,1,0:T(8,128)(2,1)S(1)} %pad_maximum_fusion), channel_id=1, source_target_pairs={{0,1},{1,2},{2,3},{4,5},{5,6},{6,7},{8,9},{9,10},{10,11},{12,13},{... | collective-permute-start | bytes 983048 | tf_op jit(solution)/shard_map/ppermute | solution.py:292
  142.8 12.6 %collective-permute-start.2 = (bf16[4,80,512]{2,1,0:T(8,128)(2,1)S(1)}, bf16[4,80,512]{2,1,0:T(8,128)(2,1)S(1)}, u32[]{:S(2)}, u32[]{:S(2)}) collective-permute-start(bf16[4,80,512]{2,1,0:T(8,128)(2,1)S(1)} %pad_maximum_fusion.1), channel_id=1, source_target_pairs={{1,0},{2,1},{3,2},{5,4},{6,5},{7,6},{9,8},{10,9},{11,10},{13,12},{... | collective-permute-start | bytes 983048 | tf_op jit(solution)/shard_map/ppermute | solution.py:292
  146.9 0.9 copy-start
  149.6 19.0 %collective-permute-start.9 = (f32[136,256]{1,0:T(8,128)}, f32[136,256]{1,0:T(8,128)S(1)}, u32[]{:S(2)}, u32[]{:S(2)}) collective-permute-start(f32[136,256]{1,0:T(8,128)} %sum.1.own_ref), channel_id=1, source_target_pairs={{0,1},{1,2},{2,3},{3,0},{4,5},{5,6},{6,7},{7,4},{8,9},{9,10},{10,1... | collective-permute-start | bytes 417800 | tf_op jit(solution)/shard_map/ppermute | solution.py:287
  150.3 18.3 %collective-permute-start.10 = (f32[136,256]{1,0:T(8,128)}, f32[136,256]{1,0:T(8,128)S(1)}, u32[]{:S(2)}, u32[]{:S(2)}) collective-permute-start(f32[136,256]{1,0:T(8,128)} %sum.1.own_ref), channel_id=1, source_target_pairs={{0,2},{1,3},{2,0},{3,1},{4,6},{5,7},{6,4},{7,5},{8,10},{9,11},{10,... | collective-permute-start | bytes 417800 | tf_op jit(solution)/shard_map/ppermute | solution.py:287
  151.1 17.5 %collective-permute-start.11 = (f32[136,256]{1,0:T(8,128)}, f32[136,256]{1,0:T(8,128)S(1)}, u32[]{:S(2)}, u32[]{:S(2)}) collective-permute-start(f32[136,256]{1,0:T(8,128)} %sum.1.own_ref), channel_id=1, source_target_pairs={{0,3},{1,0},{2,1},{3,2},{4,7},{5,4},{6,5},{7,6},{8,11},{9,8},{10,9... | collective-permute-start | bytes 417800 | tf_op jit(solution)/shard_map/ppermute | solution.py:287
  152.4 3.1 %copy-start.9 = (bf16[4,80,512]{2,1,0:T(8,128)(2,1)}, bf16[4,80,512]{2,1,0:T(8,128)(2,1)S(1)}, u32[]{:S(2)}) copy-start(bf16[4,80,512]{2,1,0:T(8,128)(2,1)S(1)} %collective-permute-done.1.low_ref) | copy-start | bytes 983044
  155.4 0.8 copy-start.11
  168.6 0.7 copy-start.6
  168.6 0.7 copy-start.7
  169.3 0.7 copy-start.8
